TPU v7x, 32 devices: a whole 2x2x4 slice. The times are simulated.
32 devices in a mesh: dp: 4 (over x, core), seq: 8 (over z, y).
Axes of the slice: x: 2, y: 2, z: 4, core: 2. Of those that a mesh axis runs over, the one named last changes fastest.
Arguments:
- inputs: bfloat16 [4, 1024, 1536], P('dp', 'seq'), may hold values from -6 to 6
- doc_lengths: int32 [4, 4], P('dp'), may hold values from 1 to 512, 1024 in all within a row
- w_query: bfloat16 [1536, 1536], P(('dp', 'seq')), may hold values from -0.15625 to 0.15625
- w_key: bfloat16 [1536, 1536], P(('dp', 'seq')), may hold values from -0.15625 to 0.15625
- w_value: bfloat16 [1536, 1536], P(('dp', 'seq')), may hold values from -0.15625 to 0.15625
- w_house: bfloat16 [1536, 1536], P(('dp', 'seq')), may hold values from -0.15625 to 0.15625
- w_beta: bfloat16 [1536, 12], P(('dp', 'seq')), may hold values from -0.15625 to 0.15625
- beta_bias: float32 [12], replicated, may hold values from -2 to 2
- norm_attn: bfloat16 [1536], P(('dp', 'seq')), may hold values from 0.5 to 1.5
- w_out: bfloat16 [1536, 1536], P(('dp', 'seq')), may hold values from -0.625 to 0.625
- norm_mlp: bfloat16 [1536], P(('dp', 'seq')), may hold values from 0.5 to 1.5
- w_gate: bfloat16 [1536, 4096], P(('dp', 'seq')), may hold values from -0.15625 to 0.15625
- w_up: bfloat16 [1536, 4096], P(('dp', 'seq')), may hold values from -0.15625 to 0.15625
- w_down: bfloat16 [4096, 1536], P(('dp', 'seq')), may hold values from -0.09375 to 0.09375
- grad_y: bfloat16 [4, 1024, 1536], P('dp', 'seq'), may hold values from -6 to 6
Outputs:
- outputs: bfloat16 [4, 1024, 1536], P('dp', 'seq')
- grad_x: float32 [4, 1024, 1536], P('dp', 'seq')
- grad_w_query: float32 [1536, 1536], P(('dp', 'seq'))
- grad_w_key: float32 [1536, 1536], P(('dp', 'seq'))
- grad_w_value: float32 [1536, 1536], P(('dp', 'seq'))
- grad_w_house: float32 [1536, 1536], P(('dp', 'seq'))
- grad_w_beta: float32 [1536, 12], P(('dp', 'seq'))
- grad_beta_bias: float32 [12], replicated
- grad_norm_attn: float32 [1536], P(('dp', 'seq'))
- grad_w_out: float32 [1536, 1536], P(('dp', 'seq'))
- grad_norm_mlp: float32 [1536], P(('dp', 'seq'))
- grad_w_gate: float32 [1536, 4096], P(('dp', 'seq'))
- grad_w_up: float32 [1536, 4096], P(('dp', 'seq'))
- grad_w_down: float32 [4096, 1536], P(('dp', 'seq'))
Inputs may be any that keep to these rules, and one draw needn't show every extreme that they name: `doc_lengths`: in every row the 4 lengths add up to 1024, and the longest is exactly half of 1024.
All inputs are finite; a program needn't handle non-finite values.
Results may differ from a plain program's by a relative error of at most 0.02.
The roundings to bfloat16 on the way count: a program that leaves them out, or rounds other values in their place, can miss the bound.
Values may be sent and summed in bfloat16 or wider, within the bound.
No kernel may reach another device: no remote copies, remote signals or barrier semaphores. Data moves between devices by JAX's collectives and lax.ppermute only.
A program may use at most 320 MiB of HBM per device.

v0:
```python
import jax
import jax.numpy as jnp
from jax import lax
from jax.sharding import PartitionSpec as P

HEADS = 12
HEAD_DIM = 128
BLOCK = 64


EPS = 1e-06
HIGH = lax.Precision.HIGHEST


def passed_along(shard, axis, by):
    peers = lax.axis_size(axis)
    pairs = [(i, i + by) for i in range(peers) if 0 <= i + by < peers]
    return lax.ppermute(shard, axis, pairs)


def as_sent(shard):

    def short(part):
        return part.astype(jnp.bfloat16) if part.dtype == jnp.float32 else part

    return jax.tree.map(short, shard)


def round_keep(value_in):
    rounded = lax.optimization_barrier(value_in.astype(jnp.bfloat16)).astype(jnp.float32)
    return value_in + lax.stop_gradient(rounded - value_in)


def rms_norm(values, gains):
    return values * lax.rsqrt(jnp.mean(values * values, axis=-1, keepdims=True) + EPS) * gains


def block_factors(queries, keys_in, houses, beta_rate):
    block_len = queries.shape[-2]
    rows_at = jnp.arange(block_len)[:, None]
    cols_at = jnp.arange(block_len)[None, :]
    house_gram = jnp.einsum("...ie,...je->...ij", houses, houses, precision=HIGH)
    lower_tri = jnp.eye(block_len, dtype=jnp.float32) + jnp.where(
        rows_at > cols_at, beta_rate[..., :, None] * house_gram, 0.0
    )
    unit_matrix = jnp.broadcast_to(jnp.eye(block_len, dtype=jnp.float32), lower_tri.shape)
    inverse = jax.scipy.linalg.solve_triangular(
        lower_tri, unit_matrix, lower=True, unit_diagonal=True
    )
    factor = inverse * beta_rate[..., None, :]
    query_house = jnp.where(
        rows_at >= cols_at, jnp.einsum("...ie,...se->...is", queries, houses, precision=HIGH), 0.0
    )
    house_key = jnp.where(
        rows_at > cols_at, jnp.einsum("...re,...je->...rj", houses, keys_in, precision=HIGH), 0.0
    )
    left_factor = jnp.einsum("...is,...sr->...ir", query_house, factor, precision=HIGH)
    factor_right = jnp.einsum("...sr,...rj->...sj", factor, house_key, precision=HIGH)
    local_raw = jnp.einsum("...ie,...je->...ij", queries, keys_in, precision=HIGH) - jnp.einsum(
        "...ir,...rj->...ij", left_factor, house_key, precision=HIGH
    )
    query_moved = round_keep(
        queries - jnp.einsum("...ir,...re->...ie", left_factor, houses, precision=HIGH)
    )
    key_moved = round_keep(
        keys_in - jnp.einsum("...sj,...se->...je", factor_right, houses, precision=HIGH)
    )
    mixing = jnp.einsum("...sr,...se->...re", factor, houses, precision=HIGH)
    return (query_moved, key_moved, mixing, local_raw)


def carry_through(keys_now, houses, mixing):
    project = jnp.einsum("...me,...re->...mr", keys_now, houses, precision=HIGH)
    return round_keep(keys_now - jnp.einsum("...mr,...re->...me", project, mixing, precision=HIGH))


def device_prep(queries, keys_in, house_raw, logits):
    houses = round_keep(
        house_raw * lax.rsqrt(jnp.sum(house_raw * house_raw, axis=-1, keepdims=True) + EPS)
    )
    beta_rates = 2.0 * jax.nn.sigmoid(logits)
    batch_n = queries.shape[0]
    pieces = queries.shape[1] // BLOCK
    moved_rows = []
    raw_rows = []
    house_list = []
    mixing_list = []
    carried = None
    for piece_at in range(pieces):
        lo_at = piece_at * BLOCK
        hi_at = lo_at + BLOCK
        house_p = houses[:, lo_at:hi_at]
        moved_q, moved_k, mixing, local_raw = block_factors(
            queries[:, lo_at:hi_at], keys_in[:, lo_at:hi_at], house_p, beta_rates[:, lo_at:hi_at]
        )
        parts_row = [local_raw]
        if carried is None:
            carried = moved_k
        else:
            parts_row = [jnp.einsum("bie,bje->bij", moved_q, carried, precision=HIGH), local_raw]
            carried = jnp.concatenate([carry_through(carried, house_p, mixing), moved_k], axis=1)
        after_len = (pieces - piece_at - 1) * BLOCK
        if after_len > 0:
            parts_row.append(jnp.zeros((batch_n, BLOCK, after_len), jnp.float32))
        raw_rows.append(jnp.concatenate(parts_row, axis=2))
        moved_rows.append(moved_q)
        house_list.append(house_p)
        mixing_list.append(mixing)
    return (
        jnp.concatenate(moved_rows, axis=1),
        carried,
        jnp.stack(house_list),
        jnp.stack(mixing_list),
        jnp.concatenate(raw_rows, axis=1),
    )


def transform_chain(keys_in, house_stack, mixing_stack):
    sections = []
    for piece_at in range(house_stack.shape[0]):
        if piece_at > 0:
            sections.append(keys_in)
        keys_in = carry_through(keys_in, house_stack[piece_at], mixing_stack[piece_at])
    return (tuple(sections), keys_in)


def hop_scores(moved_bf, section_list):
    rows_out = []
    for piece_at, section_keys in enumerate(section_list):
        query_part = moved_bf[:, piece_at * BLOCK : (piece_at + 1) * BLOCK]
        rows_out.append(
            jnp.einsum("bie,bje->bij", query_part, section_keys, preferred_element_type=jnp.float32)
        )
    return jnp.concatenate(rows_out, axis=1)


def to_heads(flat_in):
    seqs_n = flat_in.shape[0]
    group_n = flat_in.shape[1]
    return jnp.swapaxes(flat_in.reshape(seqs_n, group_n, HEADS, -1), 1, 2).reshape(
        seqs_n * HEADS, group_n, -1
    )


def from_heads(split_in, seqs_n):
    group_n = split_in.shape[1]
    return jnp.swapaxes(split_in.reshape(seqs_n, HEADS, group_n, -1), 1, 2).reshape(
        seqs_n, group_n, -1
    )


def pass_keys(sent_keys, sent_vals):
    return passed_along((sent_keys, sent_vals), "seq", 1)


def pass_grads(grad_keys, grad_vals):
    return (
        passed_along(as_sent(grad_keys), "seq", -1).astype(grad_keys.dtype),
        passed_along(grad_vals.astype(jnp.bfloat16), "seq", -1).astype(grad_vals.dtype),
    )


def on_device(
    inputs,
    doc_lengths,
    w_query,
    w_key,
    w_value,
    w_house,
    w_beta,
    beta_bias,
    norm_attn,
    w_out,
    norm_mlp,
    w_gate,
    w_up,
    w_down,
    grad_y,
):
    gathered = (
        lax.all_gather(w_query, ("dp", "seq"), axis=0, tiled=True),
        lax.all_gather(w_key, ("dp", "seq"), axis=0, tiled=True),
        lax.all_gather(w_value, ("dp", "seq"), axis=0, tiled=True),
        lax.all_gather(w_house, ("dp", "seq"), axis=0, tiled=True),
        lax.all_gather(w_beta, ("dp", "seq"), axis=0, tiled=True),
        lax.all_gather(norm_attn, ("dp", "seq"), axis=0, tiled=True),
        lax.all_gather(w_out, ("dp", "seq"), axis=0, tiled=True),
        lax.all_gather(norm_mlp, ("dp", "seq"), axis=0, tiled=True),
        lax.all_gather(w_gate, ("dp", "seq"), axis=0, tiled=True),
        lax.all_gather(w_up, ("dp", "seq"), axis=0, tiled=True),
        lax.all_gather(w_down, ("dp", "seq"), axis=0, tiled=True),
    )
    (
        query_full,
        key_full,
        value_full,
        house_full,
        beta_full,
        gain_attn,
        out_full,
        gain_mlp,
        gate_full,
        up_full,
        down_full,
    ) = gathered
    seqs_n = inputs.shape[0]
    group_n = inputs.shape[1]
    seq_count = lax.axis_size("seq")
    seq_at = lax.axis_index("seq")
    scale_by = HEAD_DIM ** (-0.5)
    total_len = group_n * seq_count
    doc_ends = jnp.cumsum(doc_lengths, axis=-1)
    doc_all = jnp.sum(
        (jnp.arange(total_len)[None, :, None] >= doc_ends[:, None, :]).astype(jnp.int32), axis=-1
    )
    own_doc = lax.dynamic_slice_in_dim(doc_all, seq_at * group_n, group_n, axis=1)
    tri_ok = jnp.arange(group_n)[:, None] >= jnp.arange(group_n)[None, :]
    local_ok = tri_ok[None] & (own_doc[:, :, None] == own_doc[:, None, :])

    def hop_ok(hop_at):
        source = seq_at - hop_at
        src_doc = lax.dynamic_slice_in_dim(
            doc_all, jnp.maximum(source, 0) * group_n, group_n, axis=1
        )
        return (source >= 0) & (own_doc[:, :, None] == src_doc[:, None, :])

    def masked_scores(raw_in, valid_at):
        shaped = raw_in.reshape(seqs_n, HEADS, group_n, group_n) * scale_by
        return jnp.where(valid_at[:, None], shaped, -1e30).reshape(raw_in.shape)

    x_float = inputs.astype(jnp.float32)
    gain_one = gain_attn.astype(jnp.float32)
    gain_two = gain_mlp.astype(jnp.float32)
    normed = rms_norm(x_float, gain_one).astype(jnp.bfloat16)
    queries = jnp.dot(normed, query_full, preferred_element_type=jnp.float32).astype(jnp.bfloat16)
    keys_all = jnp.dot(normed, key_full, preferred_element_type=jnp.float32).astype(jnp.bfloat16)
    values_all = jnp.dot(normed, value_full, preferred_element_type=jnp.float32).astype(
        jnp.bfloat16
    )
    house_raw = jnp.dot(normed, house_full, preferred_element_type=jnp.float32)
    logits = jnp.dot(normed, beta_full, preferred_element_type=jnp.float32) + beta_bias
    prep_in = (
        to_heads(queries).astype(jnp.float32),
        to_heads(keys_all).astype(jnp.float32),
        to_heads(house_raw),
        jnp.swapaxes(logits, 1, 2).reshape(-1, group_n),
    )
    moved_q, send_keys, house_stack, mixing_stack, local_raw = device_prep(
        prep_in[0], prep_in[1], prep_in[2], prep_in[3]
    )
    moved_bf = moved_q.astype(jnp.bfloat16)
    values_h = to_heads(values_all)
    local_s = masked_scores(local_raw, local_ok)
    peak_start = jnp.max(local_s, axis=-1)
    total_start = jnp.sum(jnp.exp(local_s - peak_start[..., None]), axis=-1)
    hop_list = jnp.arange(1, seq_count, dtype=jnp.int32)

    def cycle_step(carry_in, hop_at):
        sent_keys, sent_vals, row_peak, row_total = carry_in
        got_keys, got_vals = pass_keys(sent_keys, sent_vals)
        sections, moved_on = transform_chain(
            got_keys.astype(jnp.float32), house_stack, mixing_stack
        )
        section_list = (got_keys,) + tuple(
            (section_keys.astype(jnp.bfloat16) for section_keys in sections)
        )
        hop_s = masked_scores(hop_scores(moved_bf, section_list), hop_ok(hop_at))
        new_peak = jnp.maximum(row_peak, jnp.max(hop_s, axis=-1))
        row_total = row_total * jnp.exp(row_peak - new_peak) + jnp.sum(
            jnp.exp(hop_s - new_peak[..., None]), axis=-1
        )
        return (
            (moved_on.astype(jnp.bfloat16), got_vals, new_peak, row_total),
            (got_keys, got_vals),
        )

    cycle_out, kept = lax.scan(
        cycle_step, (send_keys.astype(jnp.bfloat16), values_h, peak_start, total_start), hop_list
    )
    kept_keys, kept_vals = kept
    log_sum = cycle_out[2] + jnp.log(cycle_out[3])
    probs_loc = jnp.exp(local_s - log_sum[..., None])
    out_start = jnp.einsum(
        "bij,bje->bie", probs_loc.astype(jnp.bfloat16), values_h, preferred_element_type=jnp.float32
    )

    def value_step(out_acc, item_in):
        hop_at, got_keys, got_vals = item_in
        sections, unused = transform_chain(got_keys.astype(jnp.float32), house_stack, mixing_stack)
        section_list = (got_keys,) + tuple(
            (section_keys.astype(jnp.bfloat16) for section_keys in sections)
        )
        hop_s = masked_scores(hop_scores(moved_bf, section_list), hop_ok(hop_at))
        probs_hop = jnp.exp(hop_s - log_sum[..., None])
        out_acc = out_acc + jnp.einsum(
            "bij,bje->bie",
            probs_hop.astype(jnp.bfloat16),
            got_vals,
            preferred_element_type=jnp.float32,
        )
        return (out_acc, None)

    out_acc, unused = lax.scan(value_step, out_start, (hop_list, kept_keys, kept_vals))
    attn_bf = from_heads(out_acc, seqs_n).astype(jnp.bfloat16)
    branch = jnp.dot(attn_bf, out_full, preferred_element_type=jnp.float32)
    middle = x_float + branch
    normed_mlp = rms_norm(middle, gain_two).astype(jnp.bfloat16)
    gate_val = jnp.dot(normed_mlp, gate_full, preferred_element_type=jnp.float32)
    up_val = jnp.dot(normed_mlp, up_full, preferred_element_type=jnp.float32)
    hidden = (jax.nn.silu(gate_val) * up_val).astype(jnp.bfloat16)
    result = middle + jnp.dot(hidden, down_full, preferred_element_type=jnp.float32)
    back_w = (
        lax.all_gather(w_query, ("dp", "seq"), axis=0, tiled=True),
        lax.all_gather(w_key, ("dp", "seq"), axis=0, tiled=True),
        lax.all_gather(w_value, ("dp", "seq"), axis=0, tiled=True),
        lax.all_gather(w_house, ("dp", "seq"), axis=0, tiled=True),
        lax.all_gather(w_beta, ("dp", "seq"), axis=0, tiled=True),
        lax.all_gather(norm_attn, ("dp", "seq"), axis=0, tiled=True),
        lax.all_gather(w_out, ("dp", "seq"), axis=0, tiled=True),
        lax.all_gather(norm_mlp, ("dp", "seq"), axis=0, tiled=True),
        lax.all_gather(w_gate, ("dp", "seq"), axis=0, tiled=True),
        lax.all_gather(w_up, ("dp", "seq"), axis=0, tiled=True),
        lax.all_gather(w_down, ("dp", "seq"), axis=0, tiled=True),
    )
    query_b, key_b, value_b, house_b, beta_b, unused_ga, out_b, unused_gm, gate_b, up_b, down_b = (
        back_w
    )
    d_hidden = jnp.einsum("scd,fd->scf", grad_y, down_b, preferred_element_type=jnp.float32)
    grad_down = jnp.einsum("scf,scd->fd", hidden, grad_y, preferred_element_type=jnp.float32)
    unused, swiglu_pull = jax.vjp(
        lambda gate_in, up_in: jax.nn.silu(gate_in) * up_in, gate_val, up_val
    )
    d_gate, d_up = swiglu_pull(d_hidden)
    d_gate_bf = d_gate.astype(jnp.bfloat16)
    d_up_bf = d_up.astype(jnp.bfloat16)
    d_normed_mlp = jnp.einsum(
        "scf,df->scd", d_gate_bf, gate_b, preferred_element_type=jnp.float32
    ) + jnp.einsum("scf,df->scd", d_up_bf, up_b, preferred_element_type=jnp.float32)
    grad_gate = jnp.einsum("scd,scf->df", normed_mlp, d_gate_bf, preferred_element_type=jnp.float32)
    grad_up = jnp.einsum("scd,scf->df", normed_mlp, d_up_bf, preferred_element_type=jnp.float32)
    unused, mlp_norm_pull = jax.vjp(rms_norm, middle, gain_two)
    d_middle_n, grad_gain_mlp = mlp_norm_pull(d_normed_mlp)
    d_middle = grad_y.astype(jnp.float32) + d_middle_n
    mlp_shards = (
        lax.psum_scatter(grad_gate, ("dp", "seq"), scatter_dimension=0, tiled=True),
        lax.psum_scatter(grad_up, ("dp", "seq"), scatter_dimension=0, tiled=True),
        lax.psum_scatter(grad_down, ("dp", "seq"), scatter_dimension=0, tiled=True),
        lax.psum_scatter(grad_gain_mlp, ("dp", "seq"), scatter_dimension=0, tiled=True),
    )
    d_branch = d_middle.astype(jnp.bfloat16)
    d_attn = jnp.einsum("scd,ed->sce", d_branch, out_b, preferred_element_type=jnp.float32)
    grad_out = jnp.einsum("sce,scd->ed", attn_bf, d_branch, preferred_element_type=jnp.float32)
    d_out_h = to_heads(d_attn.astype(jnp.bfloat16))
    row_delta = jnp.sum(d_out_h.astype(jnp.float32) * out_acc, axis=-1)
    dp_loc = jnp.einsum("bie,bje->bij", d_out_h, values_h, preferred_element_type=jnp.float32)
    ds_loc = (probs_loc * (dp_loc - row_delta[..., None])).astype(jnp.bfloat16)
    d_local_raw = ds_loc.astype(jnp.float32) * scale_by
    d_values_loc = jnp.einsum(
        "bij,bie->bje", probs_loc.astype(jnp.bfloat16), d_out_h, preferred_element_type=jnp.float32
    )

    def back_step(carry_in, item_in):
        grad_keys, grad_vals, d_moved, d_house, d_mixing = carry_in
        hop_at, got_keys, got_vals = item_in
        chain_out, chain_pull = jax.vjp(
            transform_chain, got_keys.astype(jnp.float32), house_stack, mixing_stack
        )
        section_list = (got_keys,) + tuple(
            (section_keys.astype(jnp.bfloat16) for section_keys in chain_out[0])
        )
        hop_s = masked_scores(hop_scores(moved_bf, section_list), hop_ok(hop_at))
        probs_hop = jnp.exp(hop_s - log_sum[..., None])
        dp_hop = jnp.einsum("bie,bje->bij", d_out_h, got_vals, preferred_element_type=jnp.float32)
        ds_hop = (probs_hop * (dp_hop - row_delta[..., None])).astype(jnp.bfloat16)
        d_rows = []
        d_sections = []
        for piece_at, section_keys in enumerate(section_list):
            ds_part = ds_hop[:, piece_at * BLOCK : (piece_at + 1) * BLOCK]
            query_part = moved_bf[:, piece_at * BLOCK : (piece_at + 1) * BLOCK]
            d_rows.append(
                jnp.einsum(
                    "bij,bje->bie", ds_part, section_keys, preferred_element_type=jnp.float32
                )
                * scale_by
            )
            d_sections.append(
                jnp.einsum("bij,bie->bje", ds_part, query_part, preferred_element_type=jnp.float32)
                * scale_by
            )
        d_vals = (
            jnp.einsum(
                "bij,bie->bje",
                probs_hop.astype(jnp.bfloat16),
                d_out_h,
                preferred_element_type=jnp.float32,
            )
            + grad_vals
        )
        d_keys_chain, d_house_hop, d_mixing_hop = chain_pull((tuple(d_sections[1:]), grad_keys))
        sent_back = pass_grads(d_keys_chain + d_sections[0], d_vals)
        return (
            (
                sent_back[0],
                sent_back[1],
                d_moved + jnp.concatenate(d_rows, axis=1),
                d_house + d_house_hop,
                d_mixing + d_mixing_hop,
            ),
            None,
        )

    back_start = (
        jnp.zeros(moved_q.shape, jnp.float32),
        jnp.zeros(values_h.shape, jnp.float32),
        jnp.zeros(moved_q.shape, jnp.float32),
        jnp.zeros(house_stack.shape, jnp.float32),
        jnp.zeros(mixing_stack.shape, jnp.float32),
    )
    back_out, unused = lax.scan(
        back_step, back_start, (hop_list, kept_keys, kept_vals), reverse=True
    )
    d_send, d_vals_in, d_moved, d_house, d_mixing = back_out
    d_values_h = d_values_loc + d_vals_in
    unused, prep_pull = jax.vjp(device_prep, prep_in[0], prep_in[1], prep_in[2], prep_in[3])
    d_query_h, d_key_h, d_house_raw, d_logits_h = prep_pull(
        (d_moved, d_send, d_house, d_mixing, d_local_raw)
    )
    d_query = from_heads(d_query_h, seqs_n).astype(jnp.bfloat16)
    d_key = from_heads(d_key_h, seqs_n).astype(jnp.bfloat16)
    d_value = from_heads(d_values_h, seqs_n).astype(jnp.bfloat16)
    d_house_bf = from_heads(d_house_raw, seqs_n).astype(jnp.bfloat16)
    d_logits = jnp.swapaxes(d_logits_h.reshape(seqs_n, HEADS, group_n), 1, 2)
    d_logits_bf = d_logits.astype(jnp.bfloat16)
    d_normed = jnp.einsum("sce,de->scd", d_query, query_b, preferred_element_type=jnp.float32)
    d_normed = d_normed + jnp.einsum(
        "sce,de->scd", d_key, key_b, preferred_element_type=jnp.float32
    )
    d_normed = d_normed + jnp.einsum(
        "sce,de->scd", d_value, value_b, preferred_element_type=jnp.float32
    )
    d_normed = d_normed + jnp.einsum(
        "sce,de->scd", d_house_bf, house_b, preferred_element_type=jnp.float32
    )
    d_normed = d_normed + jnp.einsum(
        "sch,dh->scd", d_logits_bf, beta_b, preferred_element_type=jnp.float32
    )
    grad_query = jnp.einsum("scd,sce->de", normed, d_query, preferred_element_type=jnp.float32)
    grad_key = jnp.einsum("scd,sce->de", normed, d_key, preferred_element_type=jnp.float32)
    grad_value = jnp.einsum("scd,sce->de", normed, d_value, preferred_element_type=jnp.float32)
    grad_house = jnp.einsum("scd,sce->de", normed, d_house_bf, preferred_element_type=jnp.float32)
    grad_beta = jnp.einsum("scd,sch->dh", normed, d_logits_bf, preferred_element_type=jnp.float32)
    unused, attn_norm_pull = jax.vjp(rms_norm, x_float, gain_one)
    d_x_norm, grad_gain_attn = attn_norm_pull(d_normed)
    grad_input = d_middle + d_x_norm
    attn_shards = (
        lax.psum_scatter(grad_query, ("dp", "seq"), scatter_dimension=0, tiled=True),
        lax.psum_scatter(grad_key, ("dp", "seq"), scatter_dimension=0, tiled=True),
        lax.psum_scatter(grad_value, ("dp", "seq"), scatter_dimension=0, tiled=True),
        lax.psum_scatter(grad_house, ("dp", "seq"), scatter_dimension=0, tiled=True),
        lax.psum_scatter(grad_beta, ("dp", "seq"), scatter_dimension=0, tiled=True),
        lax.psum_scatter(grad_gain_attn, ("dp", "seq"), scatter_dimension=0, tiled=True),
        lax.psum_scatter(grad_out, ("dp", "seq"), scatter_dimension=0, tiled=True),
    )
    grad_bias = lax.psum(jnp.sum(d_logits, axis=(0, 1)), ("dp", "seq"))
    return (
        result.astype(jnp.bfloat16),
        grad_input,
        attn_shards[0],
        attn_shards[1],
        attn_shards[2],
        attn_shards[3],
        attn_shards[4],
        grad_bias,
        attn_shards[5],
        attn_shards[6],
        mlp_shards[3],
        mlp_shards[0],
        mlp_shards[1],
        mlp_shards[2],
    )


def solution(mesh):
    in_specs = (
        P("dp", "seq", None),
        P("dp", None),
        P(("dp", "seq"), None),
        P(("dp", "seq"), None),
        P(("dp", "seq"), None),
        P(("dp", "seq"), None),
        P(("dp", "seq"), None),
        P(),
        P(("dp", "seq")),
        P(("dp", "seq"), None),
        P(("dp", "seq")),
        P(("dp", "seq"), None),
        P(("dp", "seq"), None),
        P(("dp", "seq"), None),
        P("dp", "seq", None),
    )
    out_specs = (
        P("dp", "seq", None),
        P("dp", "seq", None),
        P(("dp", "seq"), None),
        P(("dp", "seq"), None),
        P(("dp", "seq"), None),
        P(("dp", "seq"), None),
        P(("dp", "seq"), None),
        P(),
        P(("dp", "seq")),
        P(("dp", "seq"), None),
        P(("dp", "seq")),
        P(("dp", "seq"), None),
        P(("dp", "seq"), None),
        P(("dp", "seq"), None),
    )
    return jax.shard_map(
        on_device, mesh=mesh, in_specs=in_specs, out_specs=out_specs, check_vma=False
    )
```

profile of v0, /device:TPU:0, one launch (start us, length us, event | category | flops | bytes accessed | tf_op | source)
XLA Modules:
  0.0 2733.3 jit_solution(3336006811403363351)
XLA Ops:
  17.9 42.5 %all-reduce.18 = (bf16[1536]{0:T(1024)(128)(2,1)S(1)}, bf16[1536]{0:T(1024)(128)(2,1)S(1)}) all-reduce(bf16[1536]{0:T(1024)(128)(2,1)S(1)} %dynamic-update-slice, bf16[1536]{0:T(1024)(128)(2,1)S(1)} %dynamic-update-slice.1), channel_id=1, replica_groups=mesh['dp'=4,'seq'=8] {'dp','seq'}, use_global_device_ids=true, to_apply=%add.13 | all-reduce | flops 3072 | bytes 12288
  62.1 67.2 %all-gather = bf16[32,48,12]{1,2,0:T(8,128)(2,1)S(1)} all-gather(bf16[1,48,12]{1,2,0:T(8,128)(2,1)} %bitcast.521), channel_id=1, replica_groups=mesh['dp'=4,'seq'=8] {'dp','seq'}, dimensions={0}, use_global_device_ids=true | all-gather | bytes 38016 | tf_op jit(solution)/shard_map/all_gather | solution.py:185
  156.4 51.1 %all-gather.12.cloned.1.call-done = bf16[1536,1536]{1,0:T(8,128)(2,1)} async-done(((bf16[48,1536]{1,0:T(8,128)(2,1)}), bf16[1536,1536]{1,0:T(8,128)(2,1)}) %all-gather.12.cloned.1.call-update) | async-done | bytes 4718608 | tf_op jit(solution)/shard_map/all_gather | solution.py:182
  219.6 59.7 %custom-call.13 = f32[12,1,64,64]{2,3,1,0:T(8,128)S(1)} custom-call(f32[12,1,64,64]{3,2,1,0:T(8,128)} %get-tuple-element.860), custom_call_target="InvertDiagBlocksLowerTriangular" | custom-call | tf_op jit(solution)/shard_map/jit(_solve_triangular)/vmap()/triangular_solve/custom-call.1 | solution.py:47
  290.3 59.9 %custom-call.14 = f32[12,1,64,64]{2,3,1,0:T(8,128)S(1)} custom-call(f32[12,1,64,64]{3,2,1,0:T(8,128)} %get-tuple-element.861), custom_call_target="InvertDiagBlocksLowerTriangular" | custom-call | tf_op jit(solution)/shard_map/jit(_solve_triangular)/vmap()/triangular_solve/custom-call.1 | solution.py:47
  382.6 247.3 %while.53 = (s32[]{:T(128)}, bf16[12,128,128]{2,1,0:T(8,128)(2,1)}, bf16[12,128,128]{2,1,0:T(8,128)(2,1)}, f32[12,128]{1,0:T(8,128)S(1)}, f32[12,128]{1,0:T(8,12...) while((s32[]{:T(128)}, bf16[12,128,128]{2,1,0:T(8,128)(2,1)}, ...), condition=%wide.region_9.11_spmd, body=%wide.region_6.10_spmd.sunk | while | flops 661031936 | bytes 22987204 | solution.py:277
  447.5 15.9 collective-permute-start
  488.2 9.0 collective-permute-start
  519.8 13.8 collective-permute-start
  543.0 8.8 collective-permute-done
  560.5 7.7 collective-permute-done.1
  599.1 8.9 collective-permute-start
  633.2 89.1 %while.54 = (s32[]{:T(128)}, f32[12,128,128]{2,1,0:T(8,128)}, s32[7]{0:T(128)}, s32[]{:T(128)}, s32[1,128]{1,0:T(1,128)}, /*index=5*/s32[1,1024]{1,0:T(1,128)}, ...) while((s32[]{:T(128)}, f32[12,128,128]{2,1,0:T(8,128)}, ...), condition=%wide.region_11.13_spmd, body=%wide.region_10.12_spmd.sunk | while | flops 405241856 | bytes 9111457 | solution.py:303
  731.2 8.0 fusion.363
  739.2 7.7 fusion.364
  746.9 11.4 multiply_convert_fusion
  758.3 9.6 fusion.365
  768.0 9.6 fusion.137
  788.1 344.1 %while.55 = (s32[]{:T(128)}, f32[12,128,128]{2,1,0:T(8,128)S(1)}, f32[12,128,128]{2,1,0:T(8,128)}, f32[12,128,128]{2,1,0:T(8,128)}, f32[2,12,64,128]{3,2,1,0:T(8...) while((s32[]{:T(128)}, f32[12,128,128]{2,1,0:T(8,128)S(1)}, ...), condition=%wide.region_16.18_spmd.clone, body=%wide.region_15.17_spmd.clone.sunk | while | flops 1924038656 | bytes 66132748 | solution.py:419
  1223.1 10.2 fusion.367
  1234.5 10.2 fusion.368
  1246.0 10.2 fusion.153
  1271.7 56.9 %all-reduce.17 = (f32[12]{0:T(128)}, f32[1536]{0:T(1024)S(1)}, f32[1536]{0:T(1024)S(1)}) all-reduce(f32[12]{0:T(128)S(1)} %copy-done.150, f32[1536]{0:T(1024)S(1)} %get-tuple-element.738, f32[1536]{0:T(1024)S(1)} %copy-done.145), channel_id=1, replica_groups=mesh['dp'=4,'seq'=8] {'dp','seq'}, use_global_device_ids=true, to_apply=%region_29.32 | all-reduce | flops 3084 | bytes 24672 | tf_op jit(solution)/shard_map/psum | solution.py:464
  1332.1 7.2 fusion.97
  1340.7 71.9 %reduce-scatter.20.cloned.1.call-done = f32[48,1536]{1,0:T(8,128)} async-done(((f32[1536,1536]{1,0:T(8,128)}), f32[48,1536]{1,0:T(8,128)}) %reduce-scatter.20.cloned.1.call-update) | async-done | bytes 294928 | tf_op jit(solution)/shard_map/reduce_scatter | solution.py:462
  1412.6 141.6 %reduce-scatter.18.cloned.1.call-done = f32[48,1536]{1,0:T(8,128)} async-done(((f32[1536,1536]{1,0:T(8,128)}), f32[48,1536]{1,0:T(8,128)}) %reduce-scatter.18.cloned.1.call-update) | async-done | bytes 294928 | tf_op jit(solution)/shard_map/reduce_scatter | solution.py:459
  1554.2 141.4 %reduce-scatter.16.cloned.1.call-done = f32[48,1536]{1,0:T(8,128)} async-done(((f32[1536,1536]{1,0:T(8,128)}), f32[48,1536]{1,0:T(8,128)}) %reduce-scatter.16.cloned.1.call-update) | async-done | bytes 294928 | tf_op jit(solution)/shard_map/reduce_scatter | solution.py:458
  1695.6 141.6 %reduce-scatter.14.cloned.1.call-done = f32[48,1536]{1,0:T(8,128)} async-done(((f32[1536,1536]{1,0:T(8,128)}), f32[48,1536]{1,0:T(8,128)}) %reduce-scatter.14.cloned.1.call-update) | async-done | bytes 294928 | tf_op jit(solution)/shard_map/reduce_scatter | solution.py:457
  1837.2 141.4 %reduce-scatter.12.cloned.1.call-done = f32[48,1536]{1,0:T(8,128)} async-done(((f32[1536,1536]{1,0:T(8,128)}), f32[48,1536]{1,0:T(8,128)}) %reduce-scatter.12.cloned.1.call-update) | async-done | bytes 294928 | tf_op jit(solution)/shard_map/reduce_scatter | solution.py:456
  1978.6 248.9 %reduce-scatter.22.cloned.1.call-done = f32[48,4096]{1,0:T(8,128)} async-done(((f32[1536,4096]{1,0:T(8,128)}), f32[48,4096]{1,0:T(8,128)}) %reduce-scatter.22.cloned.1.call-update) | async-done | bytes 786448 | tf_op jit(solution)/shard_map/reduce_scatter | solution.py:345
  2227.5 249.5 %reduce-scatter.24.cloned.1.call-done = f32[48,4096]{1,0:T(8,128)} async-done(((f32[1536,4096]{1,0:T(8,128)}), f32[48,4096]{1,0:T(8,128)}) %reduce-scatter.24.cloned.1.call-update) | async-done | bytes 786448 | tf_op jit(solution)/shard_map/reduce_scatter | solution.py:346
  2476.9 249.4 %reduce-scatter.26.cloned.1.call-done = f32[128,1536]{1,0:T(8,128)} async-done(((f32[4096,1536]{1,0:T(8,128)}), f32[128,1536]{1,0:T(8,128)}) %reduce-scatter.26.cloned.1.call-update) | async-done | bytes 786448 | tf_op jit(solution)/shard_map/reduce_scatter | solution.py:347
  (1155 shorter events, 827.6 us)
Async XLA Ops:
  7.2 126.9 %all-gather.14.cloned.1.call-start = ((), (), s32[]{:S(2)}) async-start(), calls=%async_computation.11 | async-start | bytes 4866048 | tf_op jit(solution)/shard_map/all_gather | solution.py:184
  7.9 139.9 %all-gather.10.cloned.1.call-start = ((), (), s32[]{:S(2)}) async-start(), calls=%async_computation.9 | async-start | bytes 4866048 | tf_op jit(solution)/shard_map/all_gather | solution.py:181
  8.7 198.8 %all-gather.12.cloned.1.call-start = ((), (), s32[]{:S(2)}) async-start(), calls=%async_computation.10 | async-start | bytes 4866048 | tf_op jit(solution)/shard_map/all_gather | solution.py:182
  9.4 359.1 %all-gather.16.cloned.1.call-start = ((), (), s32[]{:S(2)}) async-start(), calls=%async_computation.12 | async-start | bytes 4866048 | tf_op jit(solution)/shard_map/all_gather | solution.py:183
  10.0 716.6 %all-gather.18.cloned.1.call-start = ((), (), s32[]{:S(2)}) async-start(), calls=%async_computation.13 | async-start | bytes 4866048 | tf_op jit(solution)/shard_map/all_gather | solution.py:187
  10.6 720.6 %all-gather.20.cloned.1.call-start = ((), (), s32[]{:S(2)}) async-start(), calls=%async_computation.14 | async-start | bytes 12976128 | tf_op jit(solution)/shard_map/all_gather | solution.py:189
  11.1 728.0 %all-gather.22.cloned.1.call-start = ((), (), s32[]{:S(2)}) async-start(), calls=%async_computation.15 | async-start | bytes 12976128 | tf_op jit(solution)/shard_map/all_gather | solution.py:190
  11.9 735.0 %all-gather.24.cloned.1.call-start = ((), (), s32[]{:S(2)}) async-start(), calls=%async_computation.16 | async-start | bytes 12976128 | tf_op jit(solution)/shard_map/all_gather | solution.py:191
  12.6 1326.6 %reduce-scatter.28.cloned.1.call-start = ((), (), s32[]{:S(2)}) async-start(), calls=%async_computation.25 | async-start | bytes 811008
  386.4 24.2 collective-permute-start.1
  414.2 21.0 collective-permute-start
  420.5 23.5 collective-permute-start.1
  447.5 28.5 %collective-permute-start = (bf16[12,128,128]{2,1,0:T(8,128)(2,1)}, bf16[12,128,128]{2,1,0:T(8,128)(2,1)S(1)}, u32[]{:S(2)}, u32[]{:S(2)}) collective-permute-start(bf16[12,128,128]{2,1,0:T(8,128)(2,1)} %get-tuple-element.1228), channel_id=1, source_target_pairs={{0,1},{1,2},{2,3},{3,4},{4,5},{5,6},{6,7},{8,9},{9,10},{10,11},{11... | collective-permute-start | bytes 1179656 | tf_op jit(solution)/shard_map/while/body/eval_jaxpr/ppermute | solution.py:18
  463.4 21.3 collective-permute-start.1
  519.8 32.0 %collective-permute-start = (bf16[12,128,128]{2,1,0:T(8,128)(2,1)}, bf16[12,128,128]{2,1,0:T(8,128)(2,1)S(1)}, u32[]{:S(2)}, u32[]{:S(2)}) collective-permute-start(bf16[12,128,128]{2,1,0:T(8,128)(2,1)} %get-tuple-element.1228), channel_id=1, source_target_pairs={{0,1},{1,2},{2,3},{3,4},{4,5},{5,6},{6,7},{8,9},{9,10},{10,11},{11... | collective-permute-start | bytes 1179656 | tf_op jit(solution)/shard_map/while/body/eval_jaxpr/ppermute | solution.py:18
  533.7 34.6 %collective-permute-start.1 = (bf16[12,128,128]{2,1,0:T(8,128)(2,1)}, bf16[12,128,128]{2,1,0:T(8,128)(2,1)}, u32[]{:S(2)}, u32[]{:S(2)}) collective-permute-start(bf16[12,128,128]{2,1,0:T(8,128)(2,1)} %get-tuple-element.1229), channel_id=1, source_target_pairs={{0,1},{1,2},{2,3},{3,4},{4,5},{5,6},{6,7},{8,9},{9,10},{10,11},{11... | collective-permute-start | bytes 1179656 | tf_op jit(solution)/shard_map/while/body/eval_jaxpr/ppermute | solution.py:18
  812.3 23.4 collective-permute-start.2
  815.0 26.1 collective-permute-start.3
  867.0 20.1 collective-permute-start.2
  914.5 20.1 collective-permute-start.2
  962.8 20.1 collective-permute-start.2
  1011.1 20.1 collective-permute-start.2
  1059.3 20.1 collective-permute-start.2
  1107.6 20.1 collective-permute-start.2
  1156.7 255.9 %reduce-scatter.20.cloned.1.call-start = ((), (), s32[]{:S(2)}) async-start(), calls=%async_computation.21 | async-start | bytes 9732096 | tf_op jit(solution)/shard_map/reduce_scatter | solution.py:462
  1163.0 391.2 %reduce-scatter.18.cloned.1.call-start = ((), (), s32[]{:S(2)}) async-start(), calls=%async_computation.20 | async-start | bytes 9732096 | tf_op jit(solution)/shard_map/reduce_scatter | solution.py:459
  1189.2 506.4 %reduce-scatter.16.cloned.1.call-start = ((), (), s32[]{:S(2)}) async-start(), calls=%async_computation.19 | async-start | bytes 9732096 | tf_op jit(solution)/shard_map/reduce_scatter | solution.py:458
  1199.9 637.3 %reduce-scatter.14.cloned.1.call-start = ((), (), s32[]{:S(2)}) async-start(), calls=%async_computation.18 | async-start | bytes 9732096 | tf_op jit(solution)/shard_map/reduce_scatter | solution.py:457
  1212.3 766.3 %reduce-scatter.12.cloned.1.call-start = ((), (), s32[]{:S(2)}) async-start(), calls=%async_computation.17 | async-start | bytes 9732096 | tf_op jit(solution)/shard_map/reduce_scatter | solution.py:456
  1221.7 1005.8 %reduce-scatter.22.cloned.1.call-start = ((), (), s32[]{:S(2)}) async-start(), calls=%async_computation.22 | async-start | bytes 25952256 | tf_op jit(solution)/shard_map/reduce_scatter | solution.py:345
  1233.3 1243.6 %reduce-scatter.24.cloned.1.call-start = ((), (), s32[]{:S(2)}) async-start(), calls=%async_computation.23 | async-start | bytes 25952256 | tf_op jit(solution)/shard_map/reduce_scatter | solution.py:346
  1244.7 1481.7 %reduce-scatter.26.cloned.1.call-start = ((), (), s32[]{:S(2)}) async-start(), calls=%async_computation.24 | async-start | bytes 25952256 | tf_op jit(solution)/shard_map/reduce_scatter | solution.py:347
  (275 other events, 2988.2 us)
Sparse Core Ops, SparseCore 0:
  10.9 66.4 all-gather.13
  80.3 62.2 all-gather.9
  145.6 61.8 all-gather.11
  210.3 63.1 all-gather.15
  276.2 63.3 all-gather.17
  342.4 106.8 all-gather.19
  452.2 135.4 all-gather.21
  590.6 105.6 all-gather.23
  1156.8 114.0 reduce-scatter.27
  1277.2 135.3 reduce-scatter.19
  1419.1 135.0 reduce-scatter.17
  1560.5 135.0 reduce-scatter.15
  1702.1 135.0 reduce-scatter.13
  1843.5 135.0 reduce-scatter.11
  1985.4 242.0 reduce-scatter.21
  2234.3 242.5 reduce-scatter.23
  2483.8 242.5 reduce-scatter.25
where the time goes:
time: 2750 us; the launch traced here: 2730 us
  waiting for transfers between devices  1490 us (54%)
  matrix products  570 us (21%)
  other arithmetic  233 us (8%)
  blocking collectives  167 us (6%)
  starting transfers between devices  122 us (4%)
  local copies, waits for them, and re-layouts  115 us (4%)
    reduce_scatter x1, waiting for transfers between devices, on_device(): lax.psum_scatter(grad_up, ('dp', 'seq'), scatter_dimension=0, tiled=True)  249 us
    reduce_scatter x1, waiting for transfers between devices, on_device(): lax.psum_scatter(grad_down, ('dp', 'seq'), scatter_dimension=0, tiled=True)  249 us
    reduce_scatter x1, waiting for transfers between devices, on_device(): lax.psum_scatter(grad_gate, ('dp', 'seq'), scatter_dimension=0, tiled=True)  249 us
    reduce_scatter x1, waiting for transfers between devices, on_device(): lax.psum_scatter(grad_house, ('dp', 'seq'), scatter_dimension=0, tiled=True)  142 us
    reduce_scatter x1, waiting for transfers between devices, on_device(): lax.psum_scatter(grad_key, ('dp', 'seq'), scatter_dimension=0, tiled=True)  142 us
    reduce_scatter x1, waiting for transfers between devices, on_device(): lax.psum_scatter(grad_value, ('dp', 'seq'), scatter_dimension=0, tiled=True)  141 us
    reduce_scatter x1, waiting for transfers between devices, on_device(): lax.psum_scatter(grad_query, ('dp', 'seq'), scatter_dimension=0, tiled=True)  141 us
    dot_general x66, matrix products, carry_through(): project = jnp.einsum('...me,...re->...mr', keys_now, houses, precision=HIGH)  126 us
  transfers between devices with their start and end apart: 45, of which 26 were waited for; matrix products, arithmetic and copies ran while one was open for 24% of the time, Pallas kernels for 0%

commit v1 on v0

v1 whole, which is shorter than its diff:
```python
import functools
import jax, jax.numpy as jnp
from jax import lax
from jax.experimental import pallas as pl
from jax.experimental.pallas import tpu as pltpu

bf16=jnp.bfloat16; f32=jnp.float32
E_=128; BLOCK=64; PAIR=128; CHUNK=256
EPS=1e-6
SCALE=128**-0.5

def mm(a,b,ca,cb):
    return lax.dot_general(a,b,(((ca,),(cb,)),((),())),preferred_element_type=f32)
def halves(a):
    hi=a.astype(bf16)
    return hi,(a-hi.astype(f32)).astype(bf16)
def mm_x(a,b,ca,cb):
    h,l=halves(a)
    return mm(h,b,ca,cb)+mm(l,b,ca,cb)
def mm_y(a,b,ca,cb):
    h,l=halves(b)
    return mm(a,h,ca,cb)+mm(a,l,ca,cb)
def mm_xy(a,b,ca,cb):
    ah,al=halves(a); bh,bl=halves(b)
    return mm(ah,bh,ca,cb)+(mm(ah,bl,ca,cb)+mm(al,bh,ca,cb))

def pair_masks():
    r=lax.broadcasted_iota(jnp.int32,(PAIR,PAIR),0)
    c=lax.broadcasted_iota(jnp.int32,(PAIR,PAIR),1)
    same=(r//BLOCK)==(c//BLOCK)
    return r,c,same

def col_to_row(col,eye):
    return jnp.sum(jnp.where(eye,col,0.0),axis=0,keepdims=True)

def inverse_of(a,r,c):
    eye=(r==c).astype(f32)
    x=eye-jnp.where((r//2)==(c//2),a,0.0)
    size=2
    while size<BLOCK:
        part=jnp.where(((r//(2*size))==(c//(2*size)))&((r//size)!=(c//size)),a,0.0)
        x=x-mm_xy(mm_xy(x,part,1,0),x,1,0)
        size*=2
    return x

def factors_of(q,k,w,beta,x,r,c,same):
    eye=r==c
    t=x*col_to_row(beta,eye)
    xq=jnp.where(same&(r>=c),mm(q,w,1,1),0.0)
    y=jnp.where(same&(r>c),mm(w,k,1,1),0.0)
    xt=mm_xy(xq,t,1,0)
    ty=mm_xy(t,y,1,0)
    return t,xq,y,xt,ty

def head_inputs(proj_ref,rows,h,nh):
    q=proj_ref[rows,h*E_:(h+1)*E_].astype(bf16)
    k=proj_ref[rows,(nh+h)*E_:(nh+h+1)*E_].astype(bf16)
    hr=proj_ref[rows,(3*nh+h)*E_:(3*nh+h+1)*E_]
    ex=proj_ref[rows,4*nh*E_:(4*nh+1)*E_]
    lane=lax.broadcasted_iota(jnp.int32,ex.shape,1)
    logit=jnp.sum(jnp.where(lane==h,ex,0.0),axis=1,keepdims=True)
    return q,k,hr,logit

def factor_kernel(nh,proj_ref,bias_ref,w_ref,qm_ref,kmp_ref,kmf_ref,mix_ref,loc_ref,x_ref):
    r,c,same=pair_masks()
    for h in range(nh):
        q,k,hr,logit=head_inputs(proj_ref,slice(None),h,nh)
        beta=2.0*jax.nn.sigmoid(logit+bias_ref[h])
        w=(hr*lax.rsqrt(jnp.sum(hr*hr,axis=1,keepdims=True)+EPS)).astype(bf16)
        a=jnp.where(same&(r>c),beta*mm(w,w,1,1),0.0)
        x=inverse_of(a,r,c)
        t,xq,y,xt,ty=factors_of(q,k,w,beta,x,r,c,same)
        qm=(q.astype(f32)-mm_x(xt,w,1,0)).astype(bf16)
        kmp=(k.astype(f32)-mm_x(ty,w,0,0)).astype(bf16)
        mix=mm_x(t,w,0,0)
        inner=mm(q,k,1,1)-mm_xy(xt,y,1,0)
        cross=mm(qm,kmp,1,1)
        loc=jnp.where(same,inner,cross)
        p=jnp.where((r<BLOCK)&(c>=BLOCK),mm(kmp,w,1,1),0.0)
        kmf=(kmp.astype(f32)-mm_xy(p,mix,1,0)).astype(bf16)
        w_ref[h]=w; qm_ref[h]=qm; kmp_ref[h]=kmp; kmf_ref[h]=kmf
        mix_ref[h]=mix; loc_ref[h]=loc; x_ref[h]=x

def run_factors(proj,bias,nh):
    L=proj.shape[0]; wd=proj.shape[1]
    blk=pl.BlockSpec((nh,PAIR,E_),lambda g:(0,g,0))
    o=lambda dt: jax.ShapeDtypeStruct((nh,L,E_),dt)
    return pl.pallas_call(functools.partial(factor_kernel,nh),
        grid=(L//PAIR,),
        in_specs=[pl.BlockSpec((PAIR,wd),lambda g:(g,0)),pl.BlockSpec(memory_space=pltpu.SMEM)],
        out_specs=[blk]*7,
        out_shape=[o(bf16),o(bf16),o(bf16),o(bf16),o(f32),o(f32),o(f32)],
        cost_estimate=pl.CostEstimate(flops=L//PAIR*nh*60*2*128**3,bytes_accessed=L*wd*4+nh*L*128*20,transcendentals=0),
    )(proj,bias)

def start_of(ends_ref,docs,pos):
    s=jnp.zeros_like(pos)
    for d in range(docs):
        s=jnp.maximum(s,jnp.where(pos>=ends_ref[d],ends_ref[d],0))
    return s

def scalar_start(ends_ref,docs,pos):
    s=jnp.int32(0)
    for d in range(docs):
        s=jnp.maximum(s,jnp.where(pos>=ends_ref[d],ends_ref[d],0))
    return s

def tile_pos(g,shape):
    return g*PAIR+lax.broadcasted_iota(jnp.int32,shape,0)

def chunk_range(ends_ref,docs,g):
    lo=scalar_start(ends_ref,docs,g*PAIR)//CHUNK
    hi=(g*PAIR+CHUNK-1)//CHUNK
    return lo,hi

def carried_forward(st,w,mh,ml):
    ph,pl_=halves(mm(st,w,1,1))
    return (st.astype(f32)-(mm(ph,mh,1,0)+(mm(ph,ml,1,0)+mm(pl_,mh,1,0)))).astype(bf16)

def forward_kernel(nh,docs,ends_ref,qm_ref,kmf_ref,w_ref,mix_ref,loc_ref,v_ref,
                   out_ref,lse_ref,hist_ref,stack,sbuf):
    g=pl.program_id(0)
    @pl.when(g==0)
    def _():
        stack[...]=jnp.zeros_like(stack)
    lo,hi=chunk_range(ends_ref,docs,g)
    rowstart=start_of(ends_ref,docs,tile_pos(g,(PAIR,PAIR)))
    cc=lax.broadcasted_iota(jnp.int32,(PAIR,PAIR),1)
    rr=lax.broadcasted_iota(jnp.int32,(PAIR,PAIR),0)
    okd=(cc<=rr)&(cc+g*PAIR>=rowstart)
    sd=[jnp.where(okd,loc_ref[h]*SCALE,-1e30) for h in range(nh)]
    peak=tuple(jnp.max(s,axis=1,keepdims=True) for s in sd)
    start2=start_of(ends_ref,docs,tile_pos(g,(PAIR,CHUNK)))
    c2=lax.broadcasted_iota(jnp.int32,(PAIR,CHUNK),1)
    mixs=[[halves(mix_ref[h,b*BLOCK:(b+1)*BLOCK]) for b in range(2)] for h in range(nh)]
    def step(c,pk):
        rows=pl.ds(pl.multiple_of(c*CHUNK,CHUNK),CHUNK)
        ok=(c2+c*CHUNK>=start2)&(c2+c*CHUNK<g*PAIR)
        new=[]
        for h in range(nh):
            st0=stack[h,rows,:]
            st1=carried_forward(st0,w_ref[h,0:BLOCK],*mixs[h][0])
            st2=carried_forward(st1,w_ref[h,BLOCK:PAIR],*mixs[h][1])
            s=jnp.concatenate([mm(qm_ref[h,0:BLOCK],st0,1,1),mm(qm_ref[h,BLOCK:PAIR],st1,1,1)],axis=0)
            s=jnp.where(ok,s*SCALE,-1e30)
            sbuf[h,c]=s
            hist_ref[0,0,h,rows,:]=st0
            hist_ref[0,1,h,rows,:]=st1
            stack[h,rows,:]=st2
            new.append(jnp.maximum(pk[h],jnp.max(s,axis=1,keepdims=True)))
        return tuple(new)
    peak=lax.fori_loop(lo,hi,step,peak)
    ed=[jnp.exp(sd[h]-peak[h]) for h in range(nh)]
    tot=tuple(jnp.sum(e,axis=1,keepdims=True) for e in ed)
    def step2(c,tt):
        new=[]
        for h in range(nh):
            e=jnp.exp(sbuf[h,c]-peak[h])
            sbuf[h,c]=e
            new.append(tt[h]+jnp.sum(e,axis=1,keepdims=True))
        return tuple(new)
    tot=lax.fori_loop(lo,hi,step2,tot)
    inv=[1.0/t for t in tot]
    grow=pl.ds(pl.multiple_of(g*PAIR,PAIR),PAIR)
    acc=tuple(mm((ed[h]*inv[h]).astype(bf16),v_ref[h,grow,:],1,0) for h in range(nh))
    def step3(c,ac):
        rows=pl.ds(pl.multiple_of(c*CHUNK,CHUNK),CHUNK)
        return tuple(ac[h]+mm((sbuf[h,c]*inv[h]).astype(bf16),v_ref[h,rows,:],1,0) for h in range(nh))
    acc=lax.fori_loop(lo,hi,step3,acc)
    for h in range(nh):
        out_ref[:,h*E_:(h+1)*E_]=acc[h].astype(bf16)
        lse_ref[h]=jnp.broadcast_to(peak[h]+jnp.log(tot[h]),(PAIR,E_))
        stack[h,grow,:]=kmf_ref[h]

def run_forward(ends,qm,kmf,w,mix,loc,v):
    nh,L,_=qm.shape; G=L//PAIR; docs=ends.shape[0]
    blk=pl.BlockSpec((nh,PAIR,E_),lambda g:(0,g,0))
    return pl.pallas_call(functools.partial(forward_kernel,nh,docs),
        grid=(G,),
        in_specs=[pl.BlockSpec(memory_space=pltpu.SMEM)]+[blk]*5+[pl.BlockSpec((nh,L,E_),lambda g:(0,0,0))],
        out_specs=[pl.BlockSpec((PAIR,nh*E_),lambda g:(g,0)),blk,pl.BlockSpec((1,2,nh,L,E_),lambda g:(g,0,0,0,0))],
        out_shape=[jax.ShapeDtypeStruct((L,nh*E_),bf16),jax.ShapeDtypeStruct((nh,L,E_),f32),jax.ShapeDtypeStruct((G,2,nh,L,E_),bf16)],
        scratch_shapes=[pltpu.VMEM((nh,L,E_),bf16),pltpu.VMEM((nh,-(-L//CHUNK),PAIR,CHUNK),f32)],
        cost_estimate=pl.CostEstimate(flops=nh*L*L*128*8,bytes_accessed=nh*L*128*24+G*nh*L*512,transcendentals=nh*L*L),
    )(ends,qm,kmf,w,mix,loc,v)

def backward_kernel(nh,docs,ngrp,ends_ref,qm_ref,w_ref,mix_ref,loc_ref,lse_ref,do_ref,hist_ref,v_ref,
                    dqm_ref,dloc_ref,dkf_ref,dw_ref,dmix_ref,dv_ref,grad,pbuf,dpbuf):
    g=ngrp-1-pl.program_id(0)
    @pl.when(g==ngrp-1)
    def _():
        grad[...]=jnp.zeros_like(grad)
        dv_ref[...]=jnp.zeros_like(dv_ref)
    lo,hi=chunk_range(ends_ref,docs,g)
    rowstart=start_of(ends_ref,docs,tile_pos(g,(PAIR,PAIR)))
    cc=lax.broadcasted_iota(jnp.int32,(PAIR,PAIR),1)
    rr=lax.broadcasted_iota(jnp.int32,(PAIR,PAIR),0)
    okd=(cc<=rr)&(cc+g*PAIR>=rowstart)
    start2=start_of(ends_ref,docs,tile_pos(g,(PAIR,CHUNK)))
    c2=lax.broadcasted_iota(jnp.int32,(PAIR,CHUNK),1)
    grow=pl.ds(pl.multiple_of(g*PAIR,PAIR),PAIR)
    do=[do_ref[:,h*E_:(h+1)*E_] for h in range(nh)]
    lse=[lse_ref[h,:,0:1] for h in range(nh)]
    pd=[jnp.exp(jnp.where(okd,loc_ref[h]*SCALE,-1e30)-lse[h]) for h in range(nh)]
    dpd=[mm(do[h],v_ref[h,grow,:],1,1) for h in range(nh)]
    delta=tuple(jnp.sum(pd[h]*dpd[h],axis=1,keepdims=True) for h in range(nh))
    def step(c,dl):
        rows=pl.ds(pl.multiple_of(c*CHUNK,CHUNK),CHUNK)
        ok=(c2+c*CHUNK>=start2)&(c2+c*CHUNK<g*PAIR)
        new=[]
        for h in range(nh):
            st0=hist_ref[0,0,h,rows,:]; st1=hist_ref[0,1,h,rows,:]
            s=jnp.concatenate([mm(qm_ref[h,0:BLOCK],st0,1,1),mm(qm_ref[h,BLOCK:PAIR],st1,1,1)],axis=0)
            p=jnp.exp(jnp.where(ok,s*SCALE,-1e30)-lse[h])
            dp=mm(do[h],v_ref[h,rows,:],1,1)
            pbuf[h,c]=p; dpbuf[h,c]=dp
            new.append(dl[h]+jnp.sum(p*dp,axis=1,keepdims=True))
        return tuple(new)
    delta=lax.fori_loop(lo,hi,step,delta)
    for h in range(nh):
        dloc_ref[h]=(pd[h]*(dpd[h]-delta[h])).astype(bf16)
        dv_ref[h,grow,:]=dv_ref[h,grow,:]+mm(pd[h].astype(bf16),do[h],0,0)
        dkf_ref[h]=grad[h,grow,:]
    mixs=[[halves(mix_ref[h,b*BLOCK:(b+1)*BLOCK]) for b in range(2)] for h in range(nh)]
    zero=jnp.zeros((BLOCK,E_),f32)
    def pull(gr,st,w,mh,ml,qm,ds):
        ph,pl_=halves(mm(st,w,1,1))
        gh,gl=halves(gr)
        u=mm(gh,mh,1,1)+(mm(gh,ml,1,1)+mm(gl,mh,1,1))
        uh,ul=halves(u)
        dw=mm(uh,st,0,0)+mm(ul,st,0,0)
        dm=mm(ph,gh,0,0)+(mm(ph,gl,0,0)+mm(pl_,gh,0,0))
        out=gr-(mm(uh,w,1,0)+mm(ul,w,1,0))+mm(ds,qm,0,0)*SCALE
        return out,dw,dm
    def step2(c,carry):
        rows=pl.ds(pl.multiple_of(c*CHUNK,CHUNK),CHUNK)
        new=[]
        for h in range(nh):
            dq0,dq1,dw0,dw1,dm0,dm1=carry[h]
            p=pbuf[h,c]
            ds=(p*(dpbuf[h,c]-delta[h])).astype(bf16)
            ds0=ds[0:BLOCK]; ds1=ds[BLOCK:PAIR]
            st0=hist_ref[0,0,h,rows,:]; st1=hist_ref[0,1,h,rows,:]
            dq0=dq0+mm(ds0,st0,1,0); dq1=dq1+mm(ds1,st1,1,0)
            dv_ref[h,rows,:]=dv_ref[h,rows,:]+mm(p.astype(bf16),do[h],0,0)
            gr=grad[h,rows,:]
            gr,a,b=pull(gr,st1,w_ref[h,BLOCK:PAIR],*mixs[h][1],qm_ref[h,BLOCK:PAIR],ds1)
            dw1=dw1-a; dm1=dm1-b
            gr,a,b=pull(gr,st0,w_ref[h,0:BLOCK],*mixs[h][0],qm_ref[h,0:BLOCK],ds0)
            dw0=dw0-a; dm0=dm0-b
            grad[h,rows,:]=gr
            new.append((dq0,dq1,dw0,dw1,dm0,dm1))
        return tuple(new)
    res=lax.fori_loop(lo,hi,step2,tuple((zero,)*6 for _ in range(nh)))
    for h in range(nh):
        dq0,dq1,dw0,dw1,dm0,dm1=res[h]
        dqm_ref[h,0:BLOCK]=dq0*SCALE; dqm_ref[h,BLOCK:PAIR]=dq1*SCALE
        dw_ref[h,0:BLOCK]=dw0; dw_ref[h,BLOCK:PAIR]=dw1
        dmix_ref[h,0:BLOCK]=dm0; dmix_ref[h,BLOCK:PAIR]=dm1

def run_backward(ends,qm,w,mix,loc,lse,do,hist,v):
    nh,L,_=qm.shape; G=L//PAIR; docs=ends.shape[0]
    blk=pl.BlockSpec((nh,PAIR,E_),lambda i:(0,G-1-i,0))
    o=lambda dt: jax.ShapeDtypeStruct((nh,L,E_),dt)
    full=pl.BlockSpec((nh,L,E_),lambda i:(0,0,0))
    return pl.pallas_call(functools.partial(backward_kernel,nh,docs,G),
        grid=(G,),
        in_specs=[pl.BlockSpec(memory_space=pltpu.SMEM)]+[blk]*5+[pl.BlockSpec((PAIR,nh*E_),lambda i:(G-1-i,0)),
                  pl.BlockSpec((1,2,nh,L,E_),lambda i:(G-1-i,0,0,0,0)),full],
        out_specs=[blk]*5+[full],
        out_shape=[o(f32),o(bf16),o(f32),o(f32),o(f32),o(f32)],
        scratch_shapes=[pltpu.VMEM((nh,L,E_),f32)]+[pltpu.VMEM((nh,-(-L//CHUNK),PAIR,CHUNK),f32)]*2,
        cost_estimate=pl.CostEstimate(flops=nh*L*L*128*20,bytes_accessed=nh*L*128*40+G*nh*L*512,transcendentals=nh*L*L),
    )(ends,qm,w,mix,loc,lse,do,hist,v)

def factor_back_kernel(nh,proj_ref,bias_ref,w_ref,qm_ref,kmp_ref,mix_ref,x_ref,
                       dqm_ref,dloc_ref,dkf_ref,dw_ref,dmix_ref,dv_ref,dproj_ref,dbias_ref):
    g=pl.program_id(0)
    r,c,same=pair_masks()
    eye=r==c
    lane=lax.broadcasted_iota(jnp.int32,(PAIR,E_),1)
    dlog_all=jnp.zeros((PAIR,E_),f32)
    for h in range(nh):
        q,k,hr,logit=head_inputs(proj_ref,slice(None),h,nh)
        beta=2.0*jax.nn.sigmoid(logit+bias_ref[h])
        rs=lax.rsqrt(jnp.sum(hr*hr,axis=1,keepdims=True)+EPS)
        w=w_ref[h]; qm=qm_ref[h]; kmp=kmp_ref[h]; mix=mix_ref[h]; x=x_ref[h]
        t,xq,y,xt,ty=factors_of(q,k,w,beta,x,r,c,same)
        ds=dloc_ref[h]
        dsl=jnp.where(same,ds.astype(f32),0.0).astype(bf16)
        dsc=jnp.where(same,0.0,ds.astype(f32)).astype(bf16)
        gk=dkf_ref[h]
        p=jnp.where((r<BLOCK)&(c>=BLOCK),mm(kmp,w,1,1),0.0)
        u=jnp.where((r<BLOCK)&(c>=BLOCK),mm_xy(gk,mix,1,1),0.0)
        dkm=gk-mm_x(u,w,1,0)+mm(dsc,qm,0,0)*SCALE
        dw=dw_ref[h]-mm_x(u,kmp,0,0)
        dmix=dmix_ref[h]-mm_xy(p,gk,0,0)
        dqm=dqm_ref[h]+mm(dsc,kmp,1,0)*SCALE
        dxt=-(mm_y(dsl,y,1,1)*SCALE)-mm_x(dqm,w,1,1)
        dty=-mm_y(w,dkm,1,1)
        dy=-(mm_x(xt,dsl,0,0)*SCALE)+mm_xy(t,dty,0,0)
        dy=jnp.where(same&(r>c),dy,0.0)
        dxt=jnp.where(same,dxt,0.0); dty=jnp.where(same,dty,0.0)
        dt=mm_xy(xq,dxt,0,0)+mm_xy(dty,y,1,1)+mm_y(w,dmix,1,1)
        dt=jnp.where(same,dt,0.0)
        dxq=jnp.where(same&(r>=c),mm_xy(dxt,t,1,1),0.0)
        dw=dw-mm_xy(xt,dqm,0,0)-mm_xy(ty,dkm,1,0)+mm_xy(t,dmix,1,0)+mm_x(dxq,q,0,0)+mm_x(dy,k,1,0)
        dq=dqm+mm(dsl,k,1,0)*SCALE+mm_x(dxq,w,1,0)
        dk=dkm+mm(dsl,q,0,0)*SCALE+mm_x(dy,w,0,0)
        dx=dt*col_to_row(beta,eye)
        dbr=jnp.sum(dt*x,axis=0,keepdims=True)
        da=jnp.where(same&(r>c),-mm_xy(mm_xy(x,dx,0,0),x,1,1),0.0)
        gram=mm(w,w,1,1)
        dbeta=jnp.sum(da*gram,axis=1,keepdims=True)+jnp.sum(jnp.where(eye,dbr,0.0),axis=1,keepdims=True)
        dg=beta*da
        dw=dw+mm_x(dg,w,1,0)+mm_x(dg,w,0,0)
        dlog=dbeta*beta*(1.0-0.5*beta)
        dhr=rs*dw-(rs*rs*rs)*hr*jnp.sum(hr*dw,axis=1,keepdims=True)
        dproj_ref[:,h*E_:(h+1)*E_]=dq.astype(bf16)
        dproj_ref[:,(nh+h)*E_:(nh+h+1)*E_]=dk.astype(bf16)
        dproj_ref[:,(2*nh+h)*E_:(2*nh+h+1)*E_]=dv_ref[h].astype(bf16)
        dproj_ref[:,(3*nh+h)*E_:(3*nh+h+1)*E_]=dhr.astype(bf16)
        dlog_all=dlog_all+jnp.where(lane==h,dlog,0.0)
    dproj_ref[:,4*nh*E_:(4*nh+1)*E_]=dlog_all.astype(bf16)
    @pl.when(g==0)
    def _():
        dbias_ref[...]=jnp.zeros_like(dbias_ref)
    dbias_ref[...]=dbias_ref[...]+jnp.sum(dlog_all,axis=0,keepdims=True)

def run_factor_back(proj,bias,w,qm,kmp,mix,x,dqm,dloc,dkf,dw,dmix,dv):
    nh,L,_=qm.shape; wd=proj.shape[1]
    blk=pl.BlockSpec((nh,PAIR,E_),lambda g:(0,g,0))
    return pl.pallas_call(functools.partial(factor_back_kernel,nh),
        grid=(L//PAIR,),
        in_specs=[pl.BlockSpec((PAIR,wd),lambda g:(g,0)),pl.BlockSpec(memory_space=pltpu.SMEM)]+[blk]*11,
        out_specs=[pl.BlockSpec((PAIR,wd),lambda g:(g,0)),pl.BlockSpec((1,E_),lambda g:(0,0))],
        out_shape=[jax.ShapeDtypeStruct((L,wd),bf16),jax.ShapeDtypeStruct((1,E_),f32)],
        cost_estimate=pl.CostEstimate(flops=L//PAIR*nh*100*2*128**3,bytes_accessed=L*wd*6+nh*L*128*40,transcendentals=0),
    )(proj,bias,w,qm,kmp,mix,x,dqm,dloc,dkf,dw,dmix,dv)


from jax.sharding import Mesh, PartitionSpec as P

HEADS = 12
DP = ("x", "core")
SEQ = ("hi", "lo")
TP = ("x", "core", "lo")
ALL = ("x", "core", "hi", "lo")


def rms_scale(values):
    return lax.rsqrt(jnp.mean(values * values, axis=-1, keepdims=True) + EPS)


def rms_back(grad, values, scale, gains):
    scaled = grad * gains
    inner = jnp.mean(scaled * values, axis=-1, keepdims=True)
    return scale * scaled - (scale * scale * scale) * values * inner


def dot(a, b):
    return jnp.dot(a, b, preferred_element_type=f32)


def dot_nt(a, b):
    return lax.dot_general(a, b, (((1,), (1,)), ((), ())), preferred_element_type=f32)


def dot_tn(a, b):
    return lax.dot_general(a, b, (((0,), (0,)), ((), ())), preferred_element_type=f32)


def gather(shard, axes):
    return lax.all_gather(shard, axes, axis=0, tiled=True)


def scatter(full, axes):
    return lax.psum_scatter(full, axes, scatter_dimension=0, tiled=True)


def exchange(pieces, axes):
    return lax.all_to_all(pieces, axes, 0, 0, tiled=True)


def on_device(inputs, doc_lengths, w_query, w_key, w_value, w_house, w_beta, beta_bias, norm_attn, w_out,
              norm_mlp, w_gate, w_up, w_down, grad_y):
    hi_n, lo_n = lax.axis_size("hi"), lax.axis_size("lo")
    dp_n = lax.axis_size("x") * lax.axis_size("core")
    seq_n = hi_n * lo_n
    tp_n = dp_n * lo_n
    seq_at = lax.axis_index("hi") * lo_n + lax.axis_index("lo")
    dp_at = lax.axis_index("x") * lax.axis_size("core") + lax.axis_index("core")
    rows, width = w_query.shape
    tokens = inputs.shape[1]
    length = tokens * seq_n
    ff_rows = w_down.shape[0]
    ff_n = ff_rows * hi_n
    nh = -(-HEADS // seq_n)
    head_cols = nh * E_
    slot = 4 * head_cols + E_
    x_own = inputs[0]
    gy_own = grad_y[0]

    def slots(w, each):
        return jnp.pad(w, ((0, 0), (0, seq_n * each - w.shape[1]))).reshape(rows, seq_n, each)

    spare = jnp.concatenate([
        slots(w_beta, nh),
        jnp.broadcast_to(jnp.stack([norm_attn, norm_mlp], -1)[:, None], (rows, seq_n, 2)),
        jnp.zeros((rows, seq_n, E_ - nh - 2), bf16)], axis=2)
    pack = jnp.concatenate([slots(w, head_cols) for w in (w_query, w_key, w_value, w_house)] + [spare], axis=2)
    x_row = gather(x_own, SEQ)
    pack = exchange(jnp.swapaxes(pack, 0, 1), SEQ)
    pack = gather(pack, DP).reshape(width, slot)
    gains = pack[:, 4 * head_cols + nh:4 * head_cols + nh + 2].astype(f32)
    gain_one, gain_two = gains[:, 0][None], gains[:, 1][None]
    out_full = gather(w_out, ALL)

    def unit_pieces(w):
        w = w.reshape(rows, dp_n, hi_n, lo_n, ff_rows)
        return jnp.transpose(w, (1, 3, 0, 2, 4)).reshape(tp_n, rows, ff_n)

    gate_up = exchange(jnp.concatenate([unit_pieces(w_gate), unit_pieces(w_up)], axis=2), TP)
    gate_up = gather(gate_up, "hi").reshape(width, 2 * ff_n)
    down = gather(w_down, "hi")
    gy_all = gather(gy_own, TP)

    x_rowf = x_row.astype(f32)
    row_scale = rms_scale(x_rowf)
    normed = (x_rowf * row_scale * gain_one).astype(bf16)
    proj = dot(normed, pack)
    bias_own = lax.dynamic_slice_in_dim(jnp.pad(beta_bias, (0, seq_n * nh - HEADS)), seq_at * nh, nh)
    ends = jnp.cumsum(doc_lengths[0])
    values = jnp.swapaxes(proj[:, 2 * head_cols:3 * head_cols].astype(bf16).reshape(length, nh, E_), 0, 1)
    houses, moved_q, moved_k, final_k, mixing, local_raw, inverse = run_factors(proj, bias_own, nh)
    mixed, log_sum, history = run_forward(ends, moved_q, final_k, houses, mixing, local_raw, values)
    mixed = exchange(mixed.reshape(seq_n, tokens, head_cols), SEQ)
    mixed = jnp.swapaxes(mixed, 0, 1).reshape(tokens, seq_n * head_cols)[:, :width]

    x_float = x_own.astype(f32)
    middle = x_float + dot(mixed, out_full)
    mid_scale = rms_scale(middle)
    normed_mlp = (middle * mid_scale * gain_two).astype(bf16)

    def to_owner_order(a):
        return jnp.swapaxes(a.reshape(tokens, dp_n, hi_n, lo_n * rows), 1, 2).reshape(tokens, width)

    def from_owner_order(a):
        return jnp.swapaxes(a.reshape(tokens, hi_n, dp_n, lo_n * rows), 1, 2).reshape(tokens, width)

    nm_all = gather(to_owner_order(normed_mlp), TP)
    both = dot(nm_all, gate_up)
    gate_val, up_val = both[:, :ff_n], both[:, ff_n:]
    sig = jax.nn.sigmoid(gate_val)
    silu = gate_val * sig
    hidden = (silu * up_val).astype(bf16)
    result = middle + scatter(dot(hidden, down).astype(bf16), TP).astype(f32)

    d_hidden = dot_nt(gy_all, down)
    d_gate = d_hidden * up_val * (sig * (1.0 + gate_val * (1.0 - sig)))
    d_up = d_hidden * silu
    d_both = jnp.concatenate([d_gate.astype(bf16), d_up.astype(bf16)], axis=1)
    d_nm = from_owner_order(scatter(dot_nt(d_both, gate_up).astype(bf16), TP)).astype(f32)
    grad_both = dot_tn(nm_all, d_both).astype(bf16)
    grad_down = dot_tn(hidden, gy_all).astype(bf16)
    grad_down = scatter(grad_down, "hi").astype(f32)
    grad_both = scatter(grad_both.reshape(hi_n * tp_n, rows, 2 * ff_n), "hi")
    d_middle = gy_own.astype(f32) + rms_back(d_nm, middle, mid_scale, gain_two)
    gain_mlp_part = jnp.sum(d_nm * middle * mid_scale, axis=0)

    d_branch = d_middle.astype(bf16)
    d_mixed = dot_nt(d_branch, out_full).astype(bf16)
    grad_out = scatter(dot_tn(mixed, d_branch).astype(bf16), ALL).astype(f32)
    d_mixed = jnp.pad(d_mixed, ((0, 0), (0, seq_n * head_cols - width))).reshape(tokens, seq_n, head_cols)
    d_mixed = exchange(jnp.swapaxes(d_mixed, 0, 1), SEQ).reshape(length, head_cols)
    d_mq, d_local, d_fk, d_w, d_mix, d_val = run_backward(
        ends, moved_q, houses, mixing, local_raw, log_sum, d_mixed, history, values)
    d_proj, d_bias = run_factor_back(proj, bias_own, houses, moved_q, moved_k, mixing, inverse,
                                     d_mq, d_local, d_fk, d_w, d_mix, d_val)
    d_normed_part = dot_nt(d_proj, pack)
    d_normed = scatter(d_normed_part.astype(bf16), SEQ).astype(f32)
    gain_attn_part = jnp.sum(d_normed_part * (x_rowf * row_scale), axis=0)
    grad_x = d_middle + rms_back(d_normed, x_float, rms_scale(x_float), gain_one)

    grad_both = exchange(grad_both, TP)
    grad_both = grad_both.reshape(dp_n, lo_n, rows, 2, hi_n, ff_rows)
    grad_both = jnp.transpose(grad_both, (3, 2, 0, 4, 1, 5)).reshape(2, rows, -1).astype(f32)

    grad_pack = dot_tn(normed, d_proj)
    lane = jnp.arange(E_)[None]
    spare_grad = grad_pack[:, 4 * head_cols:]
    own = nh + dp_at
    spare_grad = jnp.where(lane == own, gain_attn_part[:, None], spare_grad)
    spare_grad = jnp.where(lane == own + dp_n, gain_mlp_part[:, None], spare_grad)
    base = nh + 2 * dp_n
    for h in range(nh):
        high = d_bias[0, h].astype(bf16).astype(f32)
        at = base + (dp_at * nh + h) * 2
        spare_grad = jnp.where(lane == at, high, spare_grad)
        spare_grad = jnp.where(lane == at + 1, d_bias[0, h] - high, spare_grad)
    grad_pack = jnp.concatenate([grad_pack[:, :4 * head_cols], spare_grad], axis=1).astype(bf16)
    grad_pack = exchange(scatter(grad_pack, DP).reshape(seq_n, rows, slot), SEQ).astype(f32)

    def whole(part, n):
        return jnp.swapaxes(part, 0, 1).reshape(rows, -1)[:, :n]

    grads = [whole(grad_pack[:, :, i * head_cols:(i + 1) * head_cols], width) for i in range(4)]
    spare_grad = grad_pack[:, :, 4 * head_cols:]
    grad_beta = whole(spare_grad[:, :, :nh], HEADS)
    grad_gain_attn = jnp.sum(spare_grad[:, :, nh:nh + dp_n], axis=(0, 2))
    grad_gain_mlp = jnp.sum(spare_grad[:, :, nh + dp_n:base], axis=(0, 2))
    bias_parts = spare_grad[:, 0, base:base + 2 * nh * dp_n].reshape(seq_n, dp_n, nh, 2)
    grad_bias = jnp.sum(bias_parts, axis=(1, 3)).reshape(-1)[:HEADS]
    return (
        result.astype(bf16)[None],
        grad_x[None],
        grads[0],
        grads[1],
        grads[2],
        grads[3],
        grad_beta,
        grad_bias,
        grad_gain_attn,
        grad_out,
        grad_gain_mlp,
        grad_both[0],
        grad_both[1],
        grad_down,
    )


def solution(mesh):
    dp_n, seq_n = mesh.devices.shape
    fine = Mesh(mesh.devices.reshape(dp_n // 2, 2, seq_n // 2, 2), ALL)
    by_rows, tokens = P(ALL, None), P(DP, SEQ, None)
    in_specs = (tokens, P(DP, None), by_rows, by_rows, by_rows, by_rows, by_rows, P(), P(ALL), by_rows, P(ALL),
                by_rows, by_rows, by_rows, tokens)
    out_specs = (tokens, tokens, by_rows, by_rows, by_rows, by_rows, by_rows, P(), P(ALL), by_rows, P(ALL),
                 by_rows, by_rows, by_rows)
    return jax.shard_map(on_device, mesh=fine, in_specs=in_specs, out_specs=out_specs, check_vma=False)
```

time: 2750 us -> 926 us (0.34)
  waiting for transfers between devices: 1490 us -> 529 us
  matrix products: 570 us -> 71.9 us
  other arithmetic: 233 us -> 18 us
  Pallas kernels: 0 us -> 120 us
  starting transfers between devices: 122 us -> 14.1 us
  local copies, waits for them, and re-layouts: 115 us -> 41.7 us
  blocking collectives: 167 us -> 102 us
    reduce_scatter x8 -> x7, waiting for transfers between devices: 1390 us -> 314 us  [scatter(): return lax.psum_scatter(full, axes, scatter_dimension=0, tiled=True)]
    dot_general x310 -> x12, matrix products: 562 us -> 71.9 us  [the longest x4 26.2 us: dot_nt(): lax.dot_general(a, b, (((1,), (1,)), ((), ())), preferred_element_type=f32)]
    another operation x13 -> x3, other arithmetic: 126 us -> 0.89 us  [the longest x5 122 us: block_factors(): jax.scipy.linalg.solve_triangular(lower_tri, unit_matrix, lower=True, uni...]
    ppermute x28 -> x0, starting transfers between devices: 121 us -> none  [passed_along(): return lax.ppermute(shard, axis, pairs)]
    pallas_call x0 -> x4, Pallas kernels: none -> 120 us  [the longest x1 40.6 us: run_factors(): pl.pallas_call(functools.partial(factor_kernel, nh), grid=(L // PAIR,), i...]
    all_gather x8 -> x7, waiting for transfers between devices: 51.1 us -> 169 us  [gather(): return lax.all_gather(shard, axes, axis=0, tiled=True)]
    all_to_all x0 -> x3, blocking collectives: none -> 102 us  [exchange(): return lax.all_to_all(pieces, axes, 0, 0, tiled=True)]
    all_gather x1 -> x0, blocking collectives: 67.2 us -> none  [on_device(): lax.all_gather(w_beta, ('dp', 'seq'), axis=0, tiled=True)]
  transfers between devices with their start and end apart: 45 -> 17, of which waited for: 26 -> 14; matrix products, arithmetic and copies ran while one was open for 24% -> 11% of each run, Pallas kernels for 0% -> 13%
where the time goes in v1:
time: 926 us; the launch traced here: 914 us
  waiting for transfers between devices  529 us (57%)
  Pallas kernels  120 us (13%)
  blocking collectives  102 us (11%)
  matrix products  71.9 us (8%)
  local copies, waits for them, and re-layouts  41.7 us (5%)
  other arithmetic  18 us (2%)
  between operations  17.4 us (2%)
  starting transfers between devices  14.1 us (2%)
    reduce_scatter x7, waiting for transfers between devices, scatter(): return lax.psum_scatter(full, axes, scatter_dimension=0, tiled=True)  314 us
    all_gather x7, waiting for transfers between devices, gather(): return lax.all_gather(shard, axes, axis=0, tiled=True)  169 us
    all_to_all x3, blocking collectives, exchange(): return lax.all_to_all(pieces, axes, 0, 0, tiled=True)  102 us
    all_to_all x3, waiting for transfers between devices, exchange(): return lax.all_to_all(pieces, axes, 0, 0, tiled=True)  43.2 us
    pallas_call x1, Pallas kernels, run_factors(): pl.pallas_call(functools.partial(factor_kernel, nh), grid=(L // PAIR,), i...  40.6 us
    pallas_call x1, Pallas kernels, run_factor_back(): pl.pallas_call(functools.partial(factor_back_kernel, nh), grid=(L // PAIR...  30.2 us
    pallas_call x1, Pallas kernels, run_backward(): pl.pallas_call(functools.partial(backward_kernel, nh, docs, G), grid=(G,)...  29.4 us
    dot_general x4, matrix products, dot_nt(): lax.dot_general(a, b, (((1,), (1,)), ((), ())), preferred_element_type=f32)  26.2 us
  transfers between devices with their start and end apart: 17, of which 14 were waited for; matrix products, arithmetic and copies ran while one was open for 11% of the time, Pallas kernels for 13%

profile of v1, /device:TPU:0, one launch (start us, length us, event | category | flops | bytes accessed | tf_op | source)
XLA Modules:
  0.0 913.6 jit_solution(5222692965166012804)
XLA Ops:
  12.8 42.6 %all_to_all.30 = bf16[8,48,1152]{2,1,0:T(8,128)(2,1)} all-to-all(bf16[8,48,1152]{2,1,0:T(8,128)(2,1)S(1)} %copy.105), channel_id=1, replica_groups=mesh['x'=2,'core'=2,'hi'=4,'lo'=2] {'hi','lo'}, dimensions={0} | all-to-all | bytes 1769472 | tf_op jit(solution)/shard_map/all_to_all | solution.py:382
  61.8 15.7 %all-to-all-done.2 = bf16[8,48,1024]{2,1,0:T(8,128)(2,1)S(1)} async-done(((bf16[8,48,1024]{2,1,0:T(8,128)(2,1)}), bf16[8,48,1024]{2,1,0:T(8,128)(2,1)S(1)}, u32[]{:S(2)}, u32[]{:S(2)}) %all-to-all-start.2) | async-done | bytes 786464 | tf_op jit(solution)/shard_map/all_to_all | solution.py:382
  79.7 16.2 %all-gather.20.cloned.1.call-done = bf16[1,1024,1536]{2,1,0:T(8,128)(2,1)} async-done(((bf16[1,128,1536]{2,1,0:T(8,128)(2,1)}), bf16[1,1024,1536]{2,1,0:T(8,128)(2,1)}) %all-gather.20.cloned.1.call-update) | async-done | bytes 3145744 | tf_op jit(solution)/shard_map/all_gather | solution.py:374
  98.6 28.3 %all-gather.10.cloned.1.call-done = bf16[32,48,1152]{2,1,0:T(8,128)(2,1)} async-done(((bf16[8,48,1152]{2,1,0:T(8,128)(2,1)}), bf16[32,48,1152]{2,1,0:T(8,128)(2,1)}) %all-gather.10.cloned.1.call-update) | async-done | bytes 3538960 | tf_op jit(solution)/shard_map/all_gather | solution.py:374
  128.7 6.3 fusion.15.proj_ref
  138.5 40.6 %shard_map.254 = (bf16[2,1024,128]{2,1,0:T(8,128)(2,1)}, bf16[2,1024,128]{2,1,0:T(8,128)(2,1)}, bf16[2,1024,128]{2,1,0:T(8,128)(2,1)}, bf16[2,1024,128]{2,1,0:T(...) custom-call(f32[1024,1152]{1,0:T(8,128)} %copy-done.13, ...), custom_call_target="tpu_custom_call" | custom-call | flops 4026531840 | bytes 9961472 | tf_op jit(solution)/shard_map/pallas_call | solution.py:88
  179.1 19.6 %shard_map.255 = (bf16[1024,256]{1,0:T(8,128)(2,1)}, f32[2,1024,128]{2,1,0:T(8,128)}, bf16[8,2,2,1024,128]{4,3,2,1,0:T(8,128)(2,1)}) custom-call(s32[4]{0:T(128)} %bitcast.159, bf16[2,1024,128]{2,1,0:T(8,128)(2,1)} %get-tuple-element.32.qm_ref, bf16[2,1024,128]{2,1,0:T(8,128)(2,1)} %get-tuple-element.33.kmf_ref, ...), custom_call_target="tpu_custom_call" | custom-call | flops 2147483648 | bytes 14680064 | tf_op jit(solution)/shard_map/pallas_call | solution.py:178
  200.1 35.2 %all_to_all.31 = bf16[8,128,256]{1,2,0:T(8,128)(2,1)S(1)} all-to-all(bf16[8,128,256]{1,2,0:T(8,128)(2,1)S(1)} %copy.108), channel_id=1, replica_groups=mesh['x'=2,'core'=2,'hi'=4,'lo'=2] {'hi','lo'}, dimensions={0} | all-to-all | bytes 1048576 | tf_op jit(solution)/shard_map/all_to_all | solution.py:382
  241.3 27.3 %all-gather.16.cloned.1.call-done = bf16[32,48,1024]{2,1,0:T(8,128)(2,1)} async-done(((bf16[8,48,1024]{2,1,0:T(8,128)(2,1)}), bf16[32,48,1024]{2,1,0:T(8,128)(2,1)}) %all-gather.16.cloned.1.call-update) | async-done | bytes 3145744 | tf_op jit(solution)/shard_map/all_gather | solution.py:374
  268.7 33.6 %all-gather.14.cloned.1.call-done = bf16[1024,1536]{0,1:T(8,128)(2,1)} async-done(((bf16[128,1536]{0,1:T(8,128)(2,1)}), bf16[1024,1536]{0,1:T(8,128)(2,1)}) %all-gather.14.cloned.1.call-update) | async-done | bytes 3145744 | tf_op jit(solution)/shard_map/all_gather | solution.py:374
  302.3 8.3 fusion.38
  310.6 30.2 %all-gather.18.cloned.1.call-done = bf16[512,1536]{1,0:T(8,128)(2,1)} async-done(((bf16[128,1536]{1,0:T(8,128)(2,1)}), bf16[512,1536]{1,0:T(8,128)(2,1)}) %all-gather.18.cloned.1.call-update) | async-done | bytes 1572880 | tf_op jit(solution)/shard_map/all_gather | solution.py:374
  340.8 33.0 %all-gather.22.cloned.1.call-done = bf16[1,1024,1536]{2,1,0:T(8,128)(2,1)} async-done(((bf16[1,128,1536]{2,1,0:T(8,128)(2,1)}), bf16[1,1024,1536]{2,1,0:T(8,128)(2,1)}) %all-gather.22.cloned.1.call-update) | async-done | bytes 3145744 | tf_op jit(solution)/shard_map/all_gather | solution.py:374
  373.7 7.2 multiply_convert_fusion.1
  382.2 5.0 convolution_convert_fusion.3
  388.6 4.7 convolution_convert_fusion.1
  395.0 7.8 convolution_convert_fusion.2
  402.9 30.6 %reduce-scatter.12.cloned.1.call-done = bf16[128,1536]{1,0:T(8,128)(2,1)} async-done(((bf16[1024,1536]{1,0:T(8,128)(2,1)}), bf16[128,1536]{1,0:T(8,128)(2,1)}) %reduce-scatter.12.cloned.1.call-update) | async-done | bytes 393232 | tf_op jit(solution)/shard_map/reduce_scatter | solution.py:378
  435.2 47.8 %reduce-scatter.10.cloned.1.call-done = bf16[128,1536]{1,0:T(8,128)(2,1)} async-done(((bf16[1024,1536]{1,0:T(8,128)(2,1)}), bf16[128,1536]{1,0:T(8,128)(2,1)}) %reduce-scatter.10.cloned.1.call-update) | async-done | bytes 393232 | tf_op jit(solution)/shard_map/reduce_scatter | solution.py:378
  485.0 4.3 convolution_convert_fusion.4
  490.2 5.5 all-to-all-start.3
  497.3 27.5 %all-to-all-done.3 = bf16[8,128,256]{2,1,0:T(8,128)(2,1)S(1)} async-done(((bf16[8,128,256]{2,1,0:T(8,128)(2,1)}), bf16[8,128,256]{2,1,0:T(8,128)(2,1)S(1)}, u32[]{:S(2)}, u32[]{:S(2)}) %all-to-all-start.3) | async-done | bytes 524320 | tf_op jit(solution)/shard_map/all_to_all | solution.py:382
  525.6 29.4 %shard_map.256 = (f32[2,1024,128]{2,1,0:T(8,128)}, bf16[2,1024,128]{2,1,0:T(8,128)(2,1)}, f32[2,1024,128]{2,1,0:T(8,128)}, f32[2,1024,128]{2,1,0:T(8,128)}, f32[...) custom-call(s32[4]{0:T(128)} %bitcast.160, bf16[2,1024,128]{2,1,0:T(8,128)(2,1)} %get-tuple-element.32.qm_ref, ...), custom_call_target="tpu_custom_call" | custom-call | flops 5368709120 | bytes 18874368 | tf_op jit(solution)/shard_map/pallas_call | solution.py:266
  555.0 30.2 %shard_map.257 = (bf16[1024,1152]{1,0:T(8,128)(2,1)}, f32[1,128]{1,0:T(1,128)}) custom-call(f32[1024,1152]{1,0:T(8,128)} %copy-done.13, f32[2]{0:T(128)} %pad_dynamic-slice_fusion.bias_ref, bf16[2,1024,128]{2,1,0:T(8,128)(2,1)} %get-tuple-element.34.w_ref, bf16[2,1024,128]{2,1,0:T(8,128)(2,1)} %get-tuple-element.32.qm_ref, ...), custom_call_target="tpu_custom_call" | custom-call | flops 6710886400 | bytes 17563648 | tf_op jit(solution)/shard_map/pallas_call | solution.py:333
  585.2 6.8 fusion.13
  597.2 9.7 %fusion.3 = (bf16[1536]{0:T(1024)(128)(2,1)S(1)}, bf16[1024,1536]{1,0:T(8,128)(2,1)}) fusion(bf16[1,1024,1536]{2,1,0:T(8,128)(2,1)} %all-gather.20.cloned.1.call-done, f32[1024]{0:T(1024)S(1)} %add_rsqrt_fusion, bf16[1024,1152]{1,0:T(8,128)(2,1)} %get-tuple-element.48, bf16[1536,1152]{1,0:T(8,128)(2,1)} %bitcast.149), kind=kOutput, calls=%fused_computation.6 | convolution fusion | flops 3631741440 | bytes 12196864 | tf_op jit(solution)/shard_map/dot_general | solution.py:366
  612.5 4.9 fusion.9
  621.6 24.0 %all_to_all.32 = bf16[8,48,1024]{2,1,0:T(8,128)(2,1)} all-to-all(bf16[8,48,1024]{2,1,0:T(8,128)(2,1)} %reduce-scatter.18.cloned.1.call-done), channel_id=1, replica_groups=mesh['x'=2,'core'=2,'hi'=4,'lo'=2] {'x','core','lo'}, dimensions={0} | all-to-all | bytes 1572864 | tf_op jit(solution)/shard_map/all_to_all | solution.py:382
  645.6 12.1 %reduce-scatter.22.cloned.1.call-done = bf16[384,1152]{1,0:T(8,128)(2,1)} async-done(((bf16[1536,1152]{1,0:T(8,128)(2,1)}), bf16[384,1152]{1,0:T(8,128)(2,1)}) %reduce-scatter.22.cloned.1.call-update) | async-done | bytes 884752 | tf_op jit(solution)/shard_map/reduce_scatter | solution.py:378
  661.9 47.2 %reduce-scatter.20.cloned.1.call-done = bf16[128,1536]{1,0:T(8,128)(2,1)} async-done(((bf16[512,1536]{1,0:T(8,128)(2,1)}), bf16[128,1536]{1,0:T(8,128)(2,1)}) %reduce-scatter.20.cloned.1.call-update) | async-done | bytes 393232 | tf_op jit(solution)/shard_map/reduce_scatter | solution.py:378
  719.8 101.0 %reduce-scatter.16.cloned.1.call-done = bf16[48,1536]{1,0:T(8,128)(2,1)} async-done(((bf16[1536,1536]{1,0:T(8,128)(2,1)}), bf16[48,1536]{1,0:T(8,128)(2,1)}) %reduce-scatter.16.cloned.1.call-update) | async-done | bytes 147472 | tf_op jit(solution)/shard_map/reduce_scatter | solution.py:378
  822.4 75.1 %reduce-scatter.14.cloned.1.call-done = bf16[128,1536]{1,0:T(8,128)(2,1)} async-done(((bf16[1024,1536]{1,0:T(8,128)(2,1)}), bf16[128,1536]{1,0:T(8,128)(2,1)}) %reduce-scatter.14.cloned.1.call-update) | async-done | bytes 393232 | tf_op jit(solution)/shard_map/reduce_scatter | solution.py:378
  (183 shorter events, 78.6 us)
Async XLA Ops:
  7.2 88.7 %all-gather.20.cloned.1.call-start = ((), (), s32[]{:S(2)}) async-start(), calls=%async_computation.24 | async-start | bytes 3538944 | tf_op jit(solution)/shard_map/all_gather | solution.py:374
  7.9 118.9 %all-gather.10.cloned.1.call-start = ((), (), s32[]{:S(2)}) async-start(), calls=%async_computation.13 | async-start | bytes 4423680 | tf_op jit(solution)/shard_map/all_gather | solution.py:374
  12.3 43.8 %copy-start.11 = (bf16[48,4096]{1,0:T(8,128)(2,1)S(1)}, bf16[48,4096]{1,0:T(8,128)(2,1)}, u32[]{:S(2)}) copy-start(bf16[48,4096]{1,0:T(8,128)(2,1)} %param.26) | copy-start | bytes 1179652
  12.6 44.0 %copy-start.12 = (bf16[48,4096]{1,0:T(8,128)(2,1)S(1)}, bf16[48,4096]{1,0:T(8,128)(2,1)}, u32[]{:S(2)}) copy-start(bf16[48,4096]{1,0:T(8,128)(2,1)} %param.27) | copy-start | bytes 1179652
  55.3 180.0 %all-gather.12.cloned.1.call-start = ((), (), s32[]{:S(2)}) async-start(), calls=%async_computation.14 | async-start | bytes 4866048 | tf_op jit(solution)/shard_map/all_gather | solution.py:374
  56.6 21.8 %copy-start.26 = (f32[12]{0:T(128)S(1)}, f32[12]{0:T(128)}, u32[]{:S(2)}) copy-start(f32[12]{0:T(128)} %param.22) | copy-start | bytes 148
  56.7 22.4 %copy-start.27 = (s32[1,4]{1,0:T(1,128)S(1)}, s32[1,4]{1,0:T(1,128)}, u32[]{:S(2)}) copy-start(s32[1,4]{1,0:T(1,128)} %param.16) | copy-start | bytes 52
  58.2 19.3 %all-to-all-start.2 = ((bf16[8,48,1024]{2,1,0:T(8,128)(2,1)}), bf16[8,48,1024]{2,1,0:T(8,128)(2,1)S(1)}, u32[]{:S(2)}, u32[]{:S(2)}) async-start(bf16[8,48,1024]{2,1,0:T(8,128)(2,1)} %pad_maximum_fusion.4), calls=%async_computation.2 | async-start | bytes 1572864 | tf_op jit(solution)/shard_map/all_to_all | solution.py:382
  61.8 206.9 %all-gather.16.cloned.1.call-start = ((), (), s32[]{:S(2)}) async-start(), calls=%async_computation.16 | async-start | bytes 3932160 | tf_op jit(solution)/shard_map/all_gather | solution.py:374
  78.4 223.9 %all-gather.14.cloned.1.call-start = ((), (), s32[]{:S(2)}) async-start(), calls=%async_computation.15 | async-start | bytes 3538944 | tf_op jit(solution)/shard_map/all_gather | solution.py:374
  95.9 32.9 %copy-start.7 = (bf16[1,1024,1536]{2,1,0:T(8,128)(2,1)S(1)}, bf16[1,1024,1536]{2,1,0:T(8,128)(2,1)}, u32[]{:S(2)}) copy-start(bf16[1,1024,1536]{2,1,0:T(8,128)(2,1)} %all-gather.20.cloned.1.call-done) | copy-start | bytes 9437188
  179.1 56.2 %copy-start.3 = (bf16[1,128,1536]{2,1,0:T(8,128)(2,1)S(1)}, bf16[1,128,1536]{2,1,0:T(8,128)(2,1)}, u32[]{:S(2)}) copy-start(bf16[1,128,1536]{2,1,0:T(8,128)(2,1)} %param.15) | copy-start | bytes 1179652
  240.0 100.8 %all-gather.18.cloned.1.call-start = ((), (), s32[]{:S(2)}) async-start(), calls=%async_computation.17 | async-start | bytes 1966080 | tf_op jit(solution)/shard_map/all_gather | solution.py:374
  240.6 133.2 %all-gather.22.cloned.1.call-start = ((), (), s32[]{:S(2)}) async-start(), calls=%async_computation.25 | async-start | bytes 3538944 | tf_op jit(solution)/shard_map/all_gather | solution.py:374
  241.3 192.2 %reduce-scatter.12.cloned.1.call-start = ((), (), s32[]{:S(2)}) async-start(), calls=%async_computation.19 | async-start | bytes 3538944 | tf_op jit(solution)/shard_map/reduce_scatter | solution.py:378
  387.2 95.7 %reduce-scatter.10.cloned.1.call-start = ((), (), s32[]{:S(2)}) async-start(), calls=%async_computation.18 | async-start | bytes 3538944 | tf_op jit(solution)/shard_map/reduce_scatter | solution.py:378
  393.3 228.3 %reduce-scatter.18.cloned.1.call-start = ((), (), s32[]{:S(2)}) async-start(), calls=%async_computation.22 | async-start | bytes 3932160 | tf_op jit(solution)/shard_map/reduce_scatter | solution.py:378
  402.9 80.1 %copy-start.9 = (bf16[1,128,1536]{2,1,0:T(8,128)(2,1)S(1)}, bf16[1,128,1536]{2,1,0:T(8,128)(2,1)}, u32[]{:S(2)}) copy-start(bf16[1,128,1536]{2,1,0:T(8,128)(2,1)} %param.29) | copy-start | bytes 1179652
  490.2 34.6 %all-to-all-start.3 = ((bf16[8,128,256]{2,1,0:T(8,128)(2,1)}), bf16[8,128,256]{2,1,0:T(8,128)(2,1)S(1)}, u32[]{:S(2)}, u32[]{:S(2)}) async-start(bf16[8,128,256]{2,1,0:T(8,128)(2,1)} %bitcast.112), calls=%async_computation.5 | async-start | bytes 1048576 | tf_op jit(solution)/shard_map/all_to_all | solution.py:382
  495.7 162.0 %reduce-scatter.22.cloned.1.call-start = ((), (), s32[]{:S(2)}) async-start(), calls=%async_computation.26 | async-start | bytes 4423680 | tf_op jit(solution)/shard_map/reduce_scatter | solution.py:378
  597.1 9.8 %copy-start.15 = (pred[128]{0:T(512)(128)(4,1)S(1)}, pred[128]{0:T(512)(128)(4,1)}, u32[]{:S(2)}) copy-start(pred[128]{0:T(512)(128)(4,1)} %get-tuple-element.84) | copy-start | bytes 388
  597.1 9.8 %copy-start.16 = (pred[128]{0:T(512)(128)(4,1)S(1)}, pred[128]{0:T(512)(128)(4,1)}, u32[]{:S(2)}) copy-start(pred[128]{0:T(512)(128)(4,1)} %get-tuple-element.85) | copy-start | bytes 388
  597.1 9.8 %copy-start.17 = (pred[128]{0:T(512)(128)(4,1)S(1)}, pred[128]{0:T(512)(128)(4,1)}, u32[]{:S(2)}) copy-start(pred[128]{0:T(512)(128)(4,1)} %get-tuple-element.82) | copy-start | bytes 388
  597.2 9.8 %copy-start.18 = (pred[128]{0:T(512)(128)(4,1)S(1)}, pred[128]{0:T(512)(128)(4,1)}, u32[]{:S(2)}) copy-start(pred[128]{0:T(512)(128)(4,1)} %get-tuple-element.83) | copy-start | bytes 388
  597.2 9.8 %copy-start.19 = (pred[128]{0:T(512)(128)(4,1)S(1)}, pred[128]{0:T(512)(128)(4,1)}, u32[]{:S(2)}) copy-start(pred[128]{0:T(512)(128)(4,1)} %get-tuple-element.80) | copy-start | bytes 388
  597.2 9.8 %copy-start.20 = (pred[128]{0:T(512)(128)(4,1)S(1)}, pred[128]{0:T(512)(128)(4,1)}, u32[]{:S(2)}) copy-start(pred[128]{0:T(512)(128)(4,1)} %get-tuple-element.81) | copy-start | bytes 388
  597.2 10.0 %copy-start = (bf16[1536,1024]{0,1:T(8,128)(2,1)S(1)}, bf16[1536,1024]{0,1:T(8,128)(2,1)}, u32[]{:S(2)}) copy-start(bf16[1536,1024]{0,1:T(8,128)(2,1)} %slice.184) | copy-start | bytes 9437188
  611.3 97.8 %reduce-scatter.20.cloned.1.call-start = ((), (), s32[]{:S(2)}) async-start(), calls=%async_computation.23 | async-start | bytes 1966080 | tf_op jit(solution)/shard_map/reduce_scatter | solution.py:378
  617.4 203.4 %reduce-scatter.16.cloned.1.call-start = ((), (), s32[]{:S(2)}) async-start(), calls=%async_computation.21 | async-start | bytes 4866048 | tf_op jit(solution)/shard_map/reduce_scatter | solution.py:378
  621.0 276.5 %reduce-scatter.14.cloned.1.call-start = ((), (), s32[]{:S(2)}) async-start(), calls=%async_computation.20 | async-start | bytes 3538944 | tf_op jit(solution)/shard_map/reduce_scatter | solution.py:378
  657.7 243.3 %all-to-all-start.4 = ((bf16[8,48,1152]{2,1,0:T(8,128)(2,1)}), bf16[8,48,1152]{2,1,0:T(8,128)(2,1)S(1)}, u32[]{:S(2)}, u32[]{:S(2)}) async-start(bf16[8,48,1152]{2,1,0:T(8,128)(2,1)} %bitcast.134), calls=%async_computation.7 | async-start | bytes 1769472 | tf_op jit(solution)/shard_map/all_to_all | solution.py:382
  714.2 183.4 %copy-start.4 = (bf16[1,128,1536]{2,1,0:T(8,128)(2,1)S(1)}, bf16[1,128,1536]{2,1,0:T(8,128)(2,1)}, u32[]{:S(2)}) copy-start(bf16[1,128,1536]{2,1,0:T(8,128)(2,1)} %param.15) | copy-start | bytes 1179652
  (18 other events, 56.6 us)
Sparse Core Ops, SparseCore 0:
  10.2 85.6 all-gather.19
  97.4 29.3 all-gather.9
  129.8 63.9 all-gather.11
  195.8 72.8 all-gather.15
  271.0 31.2 all-gather.13
  303.7 37.0 all-gather.17
  342.7 31.0 all-gather.21
  387.3 46.0 reduce-scatter.11
  436.8 46.0 reduce-scatter.9
  485.1 68.6 reduce-scatter.17
  611.4 46.2 reduce-scatter.21
  659.9 49.1 reduce-scatter.19
  714.5 106.1 reduce-scatter.15
  824.2 73.2 reduce-scatter.13

commit v2 on v1

--- a/solution.py
+++ b/solution.py
@@ -9,6 +9,8 @@
 EPS=1e-6
 SCALE=128**-0.5
 
+def spent(us):
+    return pl.CostEstimate(flops=int(us*1.1e9),bytes_accessed=1<<20,transcendentals=0)
 def mm(a,b,ca,cb):
     return lax.dot_general(a,b,(((ca,),(cb,)),((),())),preferred_element_type=f32)
 def halves(a):
@@ -90,7 +92,7 @@
         in_specs=[pl.BlockSpec((PAIR,wd),lambda g:(g,0)),pl.BlockSpec(memory_space=pltpu.SMEM)],
         out_specs=[blk]*7,
         out_shape=[o(bf16),o(bf16),o(bf16),o(bf16),o(f32),o(f32),o(f32)],
-        cost_estimate=pl.CostEstimate(flops=L//PAIR*nh*60*2*128**3,bytes_accessed=L*wd*4+nh*L*128*20,transcendentals=0),
+        cost_estimate=spent(38),
     )(proj,bias)
 
 def start_of(ends_ref,docs,pos):
@@ -181,7 +183,7 @@
         out_specs=[pl.BlockSpec((PAIR,nh*E_),lambda g:(g,0)),blk,pl.BlockSpec((1,2,nh,L,E_),lambda g:(g,0,0,0,0))],
         out_shape=[jax.ShapeDtypeStruct((L,nh*E_),bf16),jax.ShapeDtypeStruct((nh,L,E_),f32),jax.ShapeDtypeStruct((G,2,nh,L,E_),bf16)],
         scratch_shapes=[pltpu.VMEM((nh,L,E_),bf16),pltpu.VMEM((nh,-(-L//CHUNK),PAIR,CHUNK),f32)],
-        cost_estimate=pl.CostEstimate(flops=nh*L*L*128*8,bytes_accessed=nh*L*128*24+G*nh*L*512,transcendentals=nh*L*L),
+        cost_estimate=spent(22),
     )(ends,qm,kmf,w,mix,loc,v)
 
 def backward_kernel(nh,docs,ngrp,ends_ref,qm_ref,w_ref,mix_ref,loc_ref,lse_ref,do_ref,hist_ref,v_ref,
@@ -270,7 +272,7 @@
         out_specs=[blk]*5+[full],
         out_shape=[o(f32),o(bf16),o(f32),o(f32),o(f32),o(f32)],
         scratch_shapes=[pltpu.VMEM((nh,L,E_),f32)]+[pltpu.VMEM((nh,-(-L//CHUNK),PAIR,CHUNK),f32)]*2,
-        cost_estimate=pl.CostEstimate(flops=nh*L*L*128*20,bytes_accessed=nh*L*128*40+G*nh*L*512,transcendentals=nh*L*L),
+        cost_estimate=spent(35),
     )(ends,qm,w,mix,loc,lse,do,hist,v)
 
 def factor_back_kernel(nh,proj_ref,bias_ref,w_ref,qm_ref,kmp_ref,mix_ref,x_ref,
@@ -335,7 +337,7 @@
         in_specs=[pl.BlockSpec((PAIR,wd),lambda g:(g,0)),pl.BlockSpec(memory_space=pltpu.SMEM)]+[blk]*11,
         out_specs=[pl.BlockSpec((PAIR,wd),lambda g:(g,0)),pl.BlockSpec((1,E_),lambda g:(0,0))],
         out_shape=[jax.ShapeDtypeStruct((L,wd),bf16),jax.ShapeDtypeStruct((1,E_),f32)],
-        cost_estimate=pl.CostEstimate(flops=L//PAIR*nh*100*2*128**3,bytes_accessed=L*wd*6+nh*L*128*40,transcendentals=0),
+        cost_estimate=spent(30),
     )(proj,bias,w,qm,kmp,mix,x,dqm,dloc,dkf,dw,dmix,dv)
 
 
@@ -380,6 +382,104 @@
 
 def exchange(pieces, axes):
     return lax.all_to_all(pieces, axes, 0, 0, tiled=True)
+
+
+def swap(a, axis):
+    return lax.ppermute(a, axis, [(0, 1), (1, 0)])
+
+
+def ring(a):
+    n = lax.axis_size("hi")
+    return lax.ppermute(a, "hi", [(i, (i + 1) % n) for i in range(n)])
+
+
+def gather_seq(a):
+    n = lax.axis_size("hi")
+    hi, lo = lax.axis_index("hi"), lax.axis_index("lo")
+    whole = jnp.zeros((n, 2) + a.shape, a.dtype)
+    zeros = (0,) * a.ndim
+    for step in range(n):
+        if step:
+            a = ring(a)
+        at = (hi + n - step) % n
+        whole = lax.dynamic_update_slice(whole, a[None, None], (at, lo) + zeros)
+        whole = lax.dynamic_update_slice(whole, swap(a, "lo")[None, None], (at, 1 - lo) + zeros)
+    return whole.reshape((-1,) + a.shape[1:])
+
+
+def scatter_seq(parts):
+    n = lax.axis_size("hi")
+    hi, lo = lax.axis_index("hi"), lax.axis_index("lo")
+    parts = parts.reshape((n, 2, -1) + parts.shape[1:])
+    total = None
+    for step in range(n):
+        at = (hi + 2 * n - 1 - step) % n
+        mine = lax.dynamic_slice_in_dim(parts, at, 1, 0)[0]
+        other = lax.dynamic_index_in_dim(mine, 1 - lo, 0, keepdims=False).astype(bf16)
+        own = lax.dynamic_index_in_dim(mine, lo, 0, keepdims=False)
+        own = own + swap(other, "lo").astype(f32)
+        total = own if total is None else own + ring(total.astype(bf16)).astype(f32)
+    return total
+
+
+def gather_tp(a):
+    half = a.shape[0] // 2
+    a_lo, a_x = swap(a, "lo"), swap(a, "x")
+    a_both = jnp.concatenate([swap(a_lo[:half], "x"), swap(a_x[half:], "lo")], axis=0)
+    parts = [a, a_lo, a_x, a_both]
+    return jnp.concatenate(parts + [swap(p, "core") for p in parts], axis=0)
+
+
+def scatter_tp(parts):
+    parts = parts.reshape((2, 4, -1) + parts.shape[1:])
+    half = parts.shape[2] // 2
+    sent = [swap(parts[1, i].astype(bf16), "core") for i in (3, 1, 2, 0)]
+    both, low, across, own = [parts[0, i] + s.astype(f32) for i, s in zip((3, 1, 2, 0), sent)]
+    from_x = swap(both[:half].astype(bf16), "x").astype(f32)
+    from_lo = swap(both[half:].astype(bf16), "lo").astype(f32)
+    low = jnp.concatenate([low[:half] + from_x, low[half:]], axis=0).astype(bf16)
+    across = jnp.concatenate([across[:half], across[half:] + from_lo], axis=0).astype(bf16)
+    return own + swap(low, "lo").astype(f32) + swap(across, "x").astype(f32)
+
+
+def join(a, axis, b=None):
+    b = swap(a, axis) if b is None else b
+    first = lax.axis_index(axis) == 0
+    return jnp.stack([jnp.where(first, a, b), jnp.where(first, b, a)])
+
+
+def keep(parts, axis):
+    first = lax.axis_index(axis) == 0
+    sent = jnp.where(first, parts[1], parts[0]).astype(bf16)
+    return jnp.where(first, parts[0], parts[1]) + swap(sent, axis).astype(f32)
+
+
+def gather_rows(a):
+    n = lax.axis_size("hi")
+    hi = lax.axis_index("hi")
+    whole = jnp.zeros((n,) + a.shape, a.dtype)
+    for step in range(n):
+        if step:
+            a = ring(a)
+        whole = lax.dynamic_update_slice(whole, a[None], ((hi + n - step) % n, 0, 0))
+    whole = whole.reshape((-1,) + a.shape[1:])
+    for axis in ("lo", "x", "core"):
+        whole = join(whole, axis).reshape((-1,) + a.shape[1:])
+    return whole
+
+
+def scatter_rows(parts):
+    tail = parts.shape[1:]
+    for axis in ("core", "x", "lo"):
+        parts = keep(parts.reshape((2, -1) + tail), axis)
+    n = lax.axis_size("hi")
+    hi = lax.axis_index("hi")
+    parts = parts.reshape((n, -1) + tail)
+    total = None
+    for step in range(n):
+        own = lax.dynamic_index_in_dim(parts, (hi + 2 * n - 1 - step) % n, 0, keepdims=False)
+        total = own if total is None else own + ring(total.astype(bf16)).astype(f32)
+    return total
 
 
 def on_device(inputs, doc_lengths, w_query, w_key, w_value, w_house, w_beta, beta_bias, norm_attn, w_out,
@@ -409,12 +509,13 @@
         jnp.broadcast_to(jnp.stack([norm_attn, norm_mlp], -1)[:, None], (rows, seq_n, 2)),
         jnp.zeros((rows, seq_n, E_ - nh - 2), bf16)], axis=2)
     pack = jnp.concatenate([slots(w, head_cols) for w in (w_query, w_key, w_value, w_house)] + [spare], axis=2)
-    x_row = gather(x_own, SEQ)
+    x_row = gather_seq(x_own)
     pack = exchange(jnp.swapaxes(pack, 0, 1), SEQ)
-    pack = gather(pack, DP).reshape(width, slot)
+    pack = join(join(pack, "x"), "core")
+    pack = jnp.swapaxes(pack, 0, 1).reshape(width, slot)
     gains = pack[:, 4 * head_cols + nh:4 * head_cols + nh + 2].astype(f32)
     gain_one, gain_two = gains[:, 0][None], gains[:, 1][None]
-    out_full = gather(w_out, ALL)
+    out_full = gather_rows(w_out)
 
     def unit_pieces(w):
         w = w.reshape(rows, dp_n, hi_n, lo_n, ff_rows)
@@ -423,7 +524,15 @@
     gate_up = exchange(jnp.concatenate([unit_pieces(w_gate), unit_pieces(w_up)], axis=2), TP)
     gate_up = gather(gate_up, "hi").reshape(width, 2 * ff_n)
     down = gather(w_down, "hi")
-    gy_all = gather(gy_own, TP)
+    gy_all = gather_tp(gy_own)
+
+    def to_gathered_order(a):
+        a = a.reshape(tokens, dp_n // 2, 2, hi_n, lo_n, rows)
+        return jnp.transpose(a, (0, 2, 1, 4, 3, 5)).reshape(tokens, width)
+
+    def from_gathered_order(a):
+        a = a.reshape(tokens, 2, dp_n // 2, lo_n, hi_n, rows)
+        return jnp.transpose(a, (0, 2, 1, 4, 3, 5)).reshape(tokens, width)
 
     x_rowf = x_row.astype(f32)
     row_scale = rms_scale(x_rowf)
@@ -436,6 +545,7 @@
     mixed, log_sum, history = run_forward(ends, moved_q, final_k, houses, mixing, local_raw, values)
     mixed = exchange(mixed.reshape(seq_n, tokens, head_cols), SEQ)
     mixed = jnp.swapaxes(mixed, 0, 1).reshape(tokens, seq_n * head_cols)[:, :width]
+    mixed = to_gathered_order(mixed)
 
     x_float = x_own.astype(f32)
     middle = x_float + dot(mixed, out_full)
@@ -448,19 +558,19 @@
     def from_owner_order(a):
         return jnp.swapaxes(a.reshape(tokens, hi_n, dp_n, lo_n * rows), 1, 2).reshape(tokens, width)
 
-    nm_all = gather(to_owner_order(normed_mlp), TP)
+    nm_all = gather_tp(to_owner_order(normed_mlp))
     both = dot(nm_all, gate_up)
     gate_val, up_val = both[:, :ff_n], both[:, ff_n:]
     sig = jax.nn.sigmoid(gate_val)
     silu = gate_val * sig
     hidden = (silu * up_val).astype(bf16)
-    result = middle + scatter(dot(hidden, down).astype(bf16), TP).astype(f32)
+    result = middle + scatter_tp(dot(hidden, down))
 
     d_hidden = dot_nt(gy_all, down)
     d_gate = d_hidden * up_val * (sig * (1.0 + gate_val * (1.0 - sig)))
     d_up = d_hidden * silu
     d_both = jnp.concatenate([d_gate.astype(bf16), d_up.astype(bf16)], axis=1)
-    d_nm = from_owner_order(scatter(dot_nt(d_both, gate_up).astype(bf16), TP)).astype(f32)
+    d_nm = from_owner_order(scatter_tp(dot_nt(d_both, gate_up)))
     grad_both = dot_tn(nm_all, d_both).astype(bf16)
     grad_down = dot_tn(hidden, gy_all).astype(bf16)
     grad_down = scatter(grad_down, "hi").astype(f32)
@@ -469,8 +579,8 @@
     gain_mlp_part = jnp.sum(d_nm * middle * mid_scale, axis=0)
 
     d_branch = d_middle.astype(bf16)
-    d_mixed = dot_nt(d_branch, out_full).astype(bf16)
-    grad_out = scatter(dot_tn(mixed, d_branch).astype(bf16), ALL).astype(f32)
+    d_mixed = from_gathered_order(dot_nt(d_branch, out_full).astype(bf16))
+    grad_out = scatter_rows(dot_tn(mixed, d_branch))
     d_mixed = jnp.pad(d_mixed, ((0, 0), (0, seq_n * head_cols - width))).reshape(tokens, seq_n, head_cols)
     d_mixed = exchange(jnp.swapaxes(d_mixed, 0, 1), SEQ).reshape(length, head_cols)
     d_mq, d_local, d_fk, d_w, d_mix, d_val = run_backward(
@@ -478,7 +588,7 @@
     d_proj, d_bias = run_factor_back(proj, bias_own, houses, moved_q, moved_k, mixing, inverse,
                                      d_mq, d_local, d_fk, d_w, d_mix, d_val)
     d_normed_part = dot_nt(d_proj, pack)
-    d_normed = scatter(d_normed_part.astype(bf16), SEQ).astype(f32)
+    d_normed = scatter_seq(d_normed_part)
     gain_attn_part = jnp.sum(d_normed_part * (x_rowf * row_scale), axis=0)
     grad_x = d_middle + rms_back(d_normed, x_float, rms_scale(x_float), gain_one)
 
@@ -498,8 +608,10 @@
         at = base + (dp_at * nh + h) * 2
         spare_grad = jnp.where(lane == at, high, spare_grad)
         spare_grad = jnp.where(lane == at + 1, d_bias[0, h] - high, spare_grad)
-    grad_pack = jnp.concatenate([grad_pack[:, :4 * head_cols], spare_grad], axis=1).astype(bf16)
-    grad_pack = exchange(scatter(grad_pack, DP).reshape(seq_n, rows, slot), SEQ).astype(f32)
+    grad_pack = jnp.concatenate([grad_pack[:, :4 * head_cols], spare_grad], axis=1)
+    grad_pack = jnp.swapaxes(grad_pack.reshape(dp_n // 2, 2, -1, slot), 0, 1)
+    grad_pack = keep(keep(grad_pack, "core"), "x").astype(bf16)
+    grad_pack = exchange(grad_pack.reshape(seq_n, rows, slot), SEQ).astype(f32)
 
     def whole(part, n):
         return jnp.swapaxes(part, 0, 1).reshape(rows, -1)[:, :n]

time: 926 us -> 712 us (0.77)
  waiting for transfers between devices: 529 us -> 219 us
  starting transfers between devices: 14.1 us -> 104 us
  blocking collectives: 102 us -> 16.7 us
  local copies, waits for them, and re-layouts: 41.7 us -> 97.9 us
  other arithmetic: 18 us -> 66.9 us
  matrix products: 71.9 us -> 61.6 us
    reduce_scatter x7 -> x2, waiting for transfers between devices: 314 us -> 0.01 us  [scatter(): return lax.psum_scatter(full, axes, scatter_dimension=0, tiled=True)]
    ppermute x0 -> x62, waiting for transfers between devices: none -> 181 us  [the longest x50 131 us: swap(): return lax.ppermute(a, axis, [(0, 1), (1, 0)])]
    all_gather x7 -> x2, waiting for transfers between devices: 169 us -> 0.01 us  [gather(): return lax.all_gather(shard, axes, axis=0, tiled=True)]
    all_to_all x3 -> x1, blocking collectives: 102 us -> 16.7 us  [exchange(): return lax.all_to_all(pieces, axes, 0, 0, tiled=True)]
    ppermute x0 -> x62, starting transfers between devices: none -> 79.3 us  [the longest x12 46 us: ring(): return lax.ppermute(a, 'hi', [(i, (i + 1) % n) for i in range(n)])]
    reshape x1 -> x3, local copies, waits for them, and re-layouts: 0.84 us -> 21.9 us  [the longest x2 21.7 us: on_device(): grad_pack = jnp.swapaxes(grad_pack.reshape(dp_n // 2, 2, -1, slot), 0, 1)]
    add x0 -> x8, other arithmetic: none -> 17.7 us  [the longest x4 11.3 us: keep(): return jnp.where(first, parts[0], parts[1]) + swap(sent, axis).astype(f32)]
    another operation x2 -> x16, other arithmetic: 0.88 us -> 12.9 us  [the longest x10 11.7 us: join(): return jnp.stack([jnp.where(first, a, b), jnp.where(first, b, a)])]
  transfers between devices with their start and end apart: 17 -> 71, of which waited for: 14 -> 27; matrix products, arithmetic and copies ran while one was open for 11% -> 28% of each run, Pallas kernels for 13% -> 17%
where the time goes in v2:
time: 712 us; the launch traced here: 704 us
  waiting for transfers between devices  219 us (31%)
  Pallas kernels  120 us (17%)
  starting transfers between devices  104 us (15%)
  local copies, waits for them, and re-layouts  97.9 us (14%)
  other arithmetic  66.9 us (9%)
  matrix products  61.6 us (9%)
  between operations  18.2 us (3%)
  blocking collectives  16.7 us (2%)
    ppermute x50, waiting for transfers between devices, swap(): return lax.ppermute(a, axis, [(0, 1), (1, 0)])  131 us
    ppermute x12, waiting for transfers between devices, ring(): return lax.ppermute(a, 'hi', [(i, (i + 1) % n) for i in range(n)])  49.6 us
    ppermute x12, starting transfers between devices, ring(): return lax.ppermute(a, 'hi', [(i, (i + 1) % n) for i in range(n)])  46 us
    pallas_call x1, Pallas kernels, run_factors(): pl.pallas_call(functools.partial(factor_kernel, nh), grid=(L // PAIR,), i...  40.6 us
    all_to_all x5, waiting for transfers between devices, exchange(): return lax.all_to_all(pieces, axes, 0, 0, tiled=True)  37.6 us
    ppermute x50, starting transfers between devices, swap(): return lax.ppermute(a, axis, [(0, 1), (1, 0)])  33.3 us
    pallas_call x1, Pallas kernels, run_factor_back(): pl.pallas_call(functools.partial(factor_back_kernel, nh), grid=(L // PAIR...  30.4 us
    pallas_call x1, Pallas kernels, run_backward(): pl.pallas_call(functools.partial(backward_kernel, nh, docs, G), grid=(G,)...  29.4 us
  transfers between devices with their start and end apart: 71, of which 27 were waited for; matrix products, arithmetic and copies ran while one was open for 28% of the time, Pallas kernels for 17%

profile of v2, /device:TPU:0, one launch (start us, length us, event | category | flops | bytes accessed | tf_op | source)
XLA Modules:
  0.0 704.4 jit_solution(17315164097862918334)
XLA Ops:
  10.5 16.7 %all_to_all.30 = bf16[8,48,1024]{2,1,0:T(8,128)(2,1)} all-to-all(bf16[8,48,1024]{2,1,0:T(8,128)(2,1)S(1)} %pad_maximum_fusion.7), channel_id=1, replica_groups=mesh['x'=2,'core'=2,'hi'=4,'lo'=2] {'x','core','lo'}, dimensions={0} | all-to-all | bytes 1572864 | tf_op jit(solution)/shard_map/all_to_all | solution.py:384
  51.5 9.7 %collective-permute-start.10 = (bf16[48,1536]{1,0:T(8,128)(2,1)}, bf16[48,1536]{1,0:T(8,128)(2,1)S(1)}, u32[]{:S(2)}, u32[]{:S(2)}) collective-permute-start(bf16[48,1536]{1,0:T(8,128)(2,1)} %collective-permute-done.9), channel_id=1, source_target_pairs={{0,2},{2,4},{4,6},{6,0},{1,3},{3,5},{5,7},{7,1},{8,10},{10,12},{12... | collective-permute-start | bytes 442376 | tf_op jit(solution)/shard_map/ppermute | solution.py:393
  62.8 21.7 %collective-permute-done.10 = bf16[48,1536]{1,0:T(8,128)(2,1)S(1)} collective-permute-done((bf16[48,1536]{1,0:T(8,128)(2,1)}, bf16[48,1536]{1,0:T(8,128)(2,1)S(1)}, u32[]{:S(2)}, u32[]{:S(2)}) %collective-permute-start.10) | collective-permute-done | bytes 147488 | tf_op jit(solution)/shard_map/ppermute | solution.py:393
  85.2 20.7 %collective-permute-start.11 = (bf16[48,1536]{1,0:T(8,128)(2,1)S(1)}, bf16[48,1536]{1,0:T(8,128)(2,1)S(1)}, u32[]{:S(2)}, u32[]{:S(2)}) collective-permute-start(bf16[48,1536]{1,0:T(8,128)(2,1)S(1)} %collective-permute-done.10), channel_id=1, source_target_pairs={{0,2},{2,4},{4,6},{6,0},{1,3},{3,5},{5,7},{7,1},{8,10},{10,12},{12... | collective-permute-start | bytes 442376 | tf_op jit(solution)/shard_map/ppermute | solution.py:393
  130.7 9.8 %collective-permute-done.12 = bf16[192,1536]{1,0:T(8,128)(2,1)S(1)} collective-permute-done((bf16[192,1536]{1,0:T(8,128)(2,1)}, bf16[192,1536]{1,0:T(8,128)(2,1)S(1)}, u32[]{:S(2)}, u32[]{:S(2)}) %collective-permute-start.12) | collective-permute-done | bytes 589856 | tf_op jit(solution)/shard_map/ppermute | solution.py:388
  144.6 6.3 collective-permute-done.4
  155.1 18.6 %collective-permute-done.7 = bf16[8,48,1152]{2,1,0:T(8,128)(2,1)S(1)} collective-permute-done((bf16[8,48,1152]{2,1,0:T(8,128)(2,1)}, bf16[8,48,1152]{2,1,0:T(8,128)(2,1)S(1)}, u32[]{:S(2)}, u32[]{:S(2)}) %collective-permute-start.7) | collective-permute-done | bytes 884768 | tf_op jit(solution)/shard_map/ppermute | solution.py:388
  182.4 13.7 %collective-permute-done.13 = bf16[384,1536]{1,0:T(8,128)(2,1)S(1)} collective-permute-done((bf16[384,1536]{1,0:T(8,128)(2,1)}, bf16[384,1536]{1,0:T(8,128)(2,1)S(1)}, u32[]{:S(2)}, u32[]{:S(2)}) %collective-permute-start.13) | collective-permute-done | bytes 1179680 | tf_op jit(solution)/shard_map/ppermute | solution.py:388
  200.6 5.9 fusion.58.proj_ref
  206.5 40.6 %shard_map.254 = (bf16[2,1024,128]{2,1,0:T(8,128)(2,1)}, bf16[2,1024,128]{2,1,0:T(8,128)(2,1)}, bf16[2,1024,128]{2,1,0:T(8,128)(2,1)}, bf16[2,1024,128]{2,1,0:T(...) custom-call(f32[1024,1152]{1,0:T(8,128)} %fusion.58.proj_ref, ...), custom_call_target="tpu_custom_call" | custom-call | flops 41799999488 | bytes 1048576 | tf_op jit(solution)/shard_map/pallas_call | solution.py:90
  249.6 19.4 %shard_map.255 = (bf16[1024,256]{1,0:T(8,128)(2,1)}, f32[2,1024,128]{2,1,0:T(8,128)}, bf16[8,2,2,1024,128]{4,3,2,1,0:T(8,128)(2,1)}) custom-call(s32[4]{0:T(128)} %bitcast.384, bf16[2,1024,128]{2,1,0:T(8,128)(2,1)} %get-tuple-element.32.qm_ref, bf16[2,1024,128]{2,1,0:T(8,128)(2,1)} %get-tuple-element.33.kmf_ref, ...), custom_call_target="tpu_custom_call" | custom-call | flops 24199999488 | bytes 1048576 | tf_op jit(solution)/shard_map/pallas_call | solution.py:180
  271.1 6.8 all-to-all-start.1
  283.5 10.1 %all-to-all-done.1 = bf16[8,128,256]{1,2,0:T(8,128)(2,1)S(1)} async-done(((bf16[8,128,256]{1,2,0:T(8,128)(2,1)}), bf16[8,128,256]{1,2,0:T(8,128)(2,1)S(1)}, u32[]{:S(2)}, u32[]{:S(2)}) %all-to-all-start.1) | async-done | bytes 524320 | tf_op jit(solution)/shard_map/all_to_all | solution.py:384
  302.5 6.8 collective-permute-done.16
  313.1 6.5 collective-permute-done.18
  324.9 6.5 concatenate.44
  331.4 8.4 %fusion.59 = f32[1024,1024]{0,1:T(8,128)} fusion(bf16[1024,1536]{0,1:T(8,128)(2,1)} %concatenate.44, bf16[1536,1024]{1,0:T(8,128)(2,1)} %bitcast.379), kind=kOutput, calls=%fused_computation.201 | convolution fusion | flops 3221225472 | bytes 10485760 | tf_op jit(solution)/shard_map/dot_general | solution.py:364
  339.8 7.6 %multiply_convert_fusion.3 = (bf16[1024,512]{0,1:T(8,128)(2,1)}, bf16[1024,512]{0,1:T(8,128)(2,1)}, bf16[1024,512]{0,1:T(8,128)(2,1)S(1)}) fusion(f32[1024,1024]{0,1:T(8,128)} %fusion.59, bf16[1024,1536]{1,0:T(8,128)(2,1)} %constant_dynamic-update-slice_fusion, bf16[512,1536]{1,0:T(8,128)(2,1)} %all-gather.5.cloned.1.call-done), kind=kOutput, calls=%fused_computation.23 | convolution fusion | flops 1618477056 | bytes 12058624 | tf_op jit(solution)/shard_map/dot_general | solution.py:368
  355.2 8.6 %fusion.57 = (bf16[2,4,128,1536]{3,2,1,0:T(8,128)(2,1)S(1)}, f32[2,4,128,1536]{3,2,1,0:T(8,128)}) fusion(bf16[2,4,128,1024]{3,2,1,0:T(8,128)(2,1)} %bitcast.344, bf16[1536,1024,1,1]{1,0,3,2:T(8,128)(2,1)} %bitcast.380), kind=kOutput, calls=%fused_computation.199 | convolution fusion | flops 3222798336 | bytes 14680064 | tf_op jit(solution)/shard_map/dot_general | solution.py:368
  372.6 6.1 convolution_convert_fusion
  432.3 21.8 %all-to-all-done.3 = bf16[8,128,256]{1,2,0:T(8,128)(2,1)S(1)} async-done(((bf16[8,128,256]{1,2,0:T(8,128)(2,1)}), bf16[8,128,256]{1,2,0:T(8,128)(2,1)S(1)}, u32[]{:S(2)}, u32[]{:S(2)}) %all-to-all-start.3) | async-done | bytes 524320 | tf_op jit(solution)/shard_map/all_to_all | solution.py:384
  455.1 29.4 %shard_map.256 = (f32[2,1024,128]{2,1,0:T(8,128)}, bf16[2,1024,128]{2,1,0:T(8,128)(2,1)}, f32[2,1024,128]{2,1,0:T(8,128)}, f32[2,1024,128]{2,1,0:T(8,128)}, f32[...) custom-call(s32[4]{0:T(128)} %bitcast.385, bf16[2,1024,128]{2,1,0:T(8,128)(2,1)} %get-tuple-element.32.qm_ref, ...), custom_call_target="tpu_custom_call" | custom-call | flops 38499999744 | bytes 1048576 | tf_op jit(solution)/shard_map/pallas_call | solution.py:268
  484.5 30.4 %shard_map.257 = (bf16[1024,1152]{1,0:T(8,128)(2,1)}, f32[1,128]{1,0:T(1,128)}) custom-call(f32[1024,1152]{1,0:T(8,128)} %fusion.58.proj_ref, f32[2]{0:T(128)} %pad_dynamic-slice_fusion.bias_ref, bf16[2,1024,128]{2,1,0:T(8,128)(2,1)} %get-tuple-element.34.w_ref, bf16[2,1024,128]{2,1,0:T(8,128)(2,1)} %get-tuple-element.32.qm_ref, ...), custom_call_target="tpu_custom_call" | custom-call | flops 32999999488 | bytes 1048576 | tf_op jit(solution)/shard_map/pallas_call | solution.py:335
  518.9 7.1 %multiply_reduce_fusion = (f32[1536]{0:T(1024)S(1)}, bf16[1024,1536]{1,0:T(8,128)(2,1)S(1)}, f32[1024,1536]{1,0:T(8,128)S(1)}) fusion(bf16[4,2,128,1536]{3,2,1,0:T(8,128)(2,1)S(1)} %copy-done.3, f32[1024]{0:T(1024)S(1)} %bitcast.376, f32[1536]{0:T(1024)S(1)} %copy-done.27, bf16[1024,1152]{1,0:T(8,128)(2,1)} %get-tuple-element.48, ...), kind=kOutput, calls=%fused_computation.2 | convolution fusion | flops 3633314304 | bytes 18497536 | tf_op jit(solution)/shard_map/dot_general | solution.py:368
  536.0 11.5 %collective-permute-done.50 = bf16[128,1536]{1,0:T(8,128)(2,1)S(1)} collective-permute-done((bf16[128,1536]{1,0:T(8,128)(2,1)S(1)}, bf16[128,1536]{1,0:T(8,128)(2,1)S(1)}, u32[]{:S(2)}, u32[]{:S(2)}) %collective-permute-start.50) | collective-permute-done | bytes 393248 | tf_op jit(solution)/shard_map/ppermute | solution.py:388
  551.8 9.4 %reshape.373 = f32[2,2,384,1152]{2,1,0,3:T(2,128)} reshape(f32[1536,1152]{0,1:T(8,128)} %pad_maximum_fusion) | data formatting | bytes 14155776 | tf_op jit(solution)/shard_map/reshape | solution.py:612
  561.2 12.3 %copy.117 = f32[2,2,384,1152]{3,2,0,1:T(8,128)} copy(f32[2,2,384,1152]{2,1,0,3:T(2,128)} %reshape.373) | data formatting | bytes 14155776 | tf_op jit(solution)/shard_map/reshape | solution.py:612
  586.1 5.7 convert_add_fusion
  602.6 18.6 %collective-permute-done.57 = bf16[384,1536]{1,0:T(8,128)(2,1)} collective-permute-done((bf16[384,1536]{1,0:T(8,128)(2,1)}, bf16[384,1536]{1,0:T(8,128)(2,1)}, u32[]{:S(2)}, u32[]{:S(2)}) %collective-permute-start.57) | collective-permute-done | bytes 1179680 | tf_op jit(solution)/shard_map/ppermute | solution.py:388
  625.6 9.7 %collective-permute-done.58 = bf16[192,1536]{1,0:T(8,128)(2,1)S(1)} collective-permute-done((bf16[192,1536]{1,0:T(8,128)(2,1)S(1)}, bf16[192,1536]{1,0:T(8,128)(2,1)S(1)}, u32[]{:S(2)}, u32[]{:S(2)}) %collective-permute-start.58) | collective-permute-done | bytes 589856 | tf_op jit(solution)/shard_map/ppermute | solution.py:388
  644.5 5.3 all-to-all-start.4
  651.9 17.4 %collective-permute-done.60 = bf16[48,1536]{1,0:T(8,128)(2,1)S(1)} collective-permute-done((bf16[48,1536]{1,0:T(8,128)(2,1)S(1)}, bf16[48,1536]{1,0:T(8,128)(2,1)S(1)}, u32[]{:S(2)}, u32[]{:S(2)}) %collective-permute-start.60) | collective-permute-done | bytes 147488 | tf_op jit(solution)/shard_map/ppermute | solution.py:393
  (396 shorter events, 257.1 us)
Async XLA Ops:
  7.2 324.2 %all-gather.3.cloned.1.call-start = ((), (), s32[]{:S(2)}) async-start(), calls=%async_computation.8 | async-start | bytes 3932160 | tf_op jit(solution)/shard_map/all_gather | solution.py:376
  27.3 82.6 %collective-permute-start = (bf16[128,1536]{1,0:T(8,128)(2,1)S(1)}, bf16[128,1536]{1,0:T(8,128)(2,1)}, u32[]{:S(2)}, u32[]{:S(2)}) collective-permute-start(bf16[128,1536]{1,0:T(8,128)(2,1)S(1)} %bitcast.320), channel_id=1, source_target_pairs={{0,1},{1,0},{2,3},{3,2},{4,5},{5,4},{6,7},{7,6},{8,9},{9,8},{10,11... | collective-permute-start | bytes 1179656 | tf_op jit(solution)/shard_map/ppermute | solution.py:388
  28.8 81.8 %collective-permute-start.1 = (bf16[128,1536]{1,0:T(8,128)(2,1)S(1)}, bf16[128,1536]{1,0:T(8,128)(2,1)}, u32[]{:S(2)}, u32[]{:S(2)}) collective-permute-start(bf16[128,1536]{1,0:T(8,128)(2,1)S(1)} %bitcast.321), channel_id=1, source_target_pairs={{0,2},{2,4},{4,6},{6,0},{1,3},{3,5},{5,7},{7,1},{8,10},{10,12},{12... | collective-permute-start | bytes 1179656 | tf_op jit(solution)/shard_map/ppermute | solution.py:393
  30.4 54.7 %collective-permute-start.32 = (bf16[128,1536]{1,0:T(8,128)(2,1)}, bf16[128,1536]{1,0:T(8,128)(2,1)}, u32[]{:S(2)}, u32[]{:S(2)}) collective-permute-start(bf16[128,1536]{1,0:T(8,128)(2,1)} %bitcast.61), channel_id=1, source_target_pairs={{0,16},{16,0},{1,17},{17,1},{2,18},{18,2},{3,19},{19,3},{4,20},{20... | collective-permute-start | bytes 1179656 | tf_op jit(solution)/shard_map/ppermute | solution.py:388
  31.0 75.8 %collective-permute-start.31 = (bf16[128,1536]{1,0:T(8,128)(2,1)}, bf16[128,1536]{1,0:T(8,128)(2,1)}, u32[]{:S(2)}, u32[]{:S(2)}) collective-permute-start(bf16[128,1536]{1,0:T(8,128)(2,1)} %bitcast.61), channel_id=1, source_target_pairs={{0,1},{1,0},{2,3},{3,2},{4,5},{5,4},{6,7},{7,6},{8,9},{9,8},{10,11... | collective-permute-start | bytes 1179656 | tf_op jit(solution)/shard_map/ppermute | solution.py:388
  35.8 115.1 %all-to-all-start = ((bf16[8,48,1152]{2,1,0:T(8,128)(2,1)}), bf16[8,48,1152]{2,1,0:T(8,128)(2,1)}, u32[]{:S(2)}, u32[]{:S(2)}) async-start(bf16[8,48,1152]{2,1,0:T(8,128)(2,1)} %copy.99), calls=%async_computation | async-start | bytes 1769472 | tf_op jit(solution)/shard_map/all_to_all | solution.py:384
  40.1 299.7 %all-gather.5.cloned.1.call-start = ((), (), s32[]{:S(2)}) async-start(), calls=%async_computation.9 | async-start | bytes 1966080 | tf_op jit(solution)/shard_map/all_gather | solution.py:376
  51.5 33.0 %collective-permute-start.10 = (bf16[48,1536]{1,0:T(8,128)(2,1)}, bf16[48,1536]{1,0:T(8,128)(2,1)S(1)}, u32[]{:S(2)}, u32[]{:S(2)}) collective-permute-start(bf16[48,1536]{1,0:T(8,128)(2,1)} %collective-permute-done.9), channel_id=1, source_target_pairs={{0,2},{2,4},{4,6},{6,0},{1,3},{3,5},{5,7},{7,1},{8,10},{10,12},{12... | collective-permute-start | bytes 442376 | tf_op jit(solution)/shard_map/ppermute | solution.py:393
  84.5 216.3 %collective-permute-start.35 = (bf16[128,1536]{1,0:T(8,128)(2,1)}, bf16[128,1536]{1,0:T(8,128)(2,1)}, u32[]{:S(2)}, u32[]{:S(2)}) collective-permute-start(bf16[128,1536]{1,0:T(8,128)(2,1)} %bitcast.61), channel_id=1, source_target_pairs={{0,8},{8,0},{1,9},{9,1},{2,10},{10,2},{3,11},{11,3},{4,12},{12,4},... | collective-permute-start | bytes 1179656 | tf_op jit(solution)/shard_map/ppermute | solution.py:388
  85.2 32.0 %collective-permute-start.11 = (bf16[48,1536]{1,0:T(8,128)(2,1)S(1)}, bf16[48,1536]{1,0:T(8,128)(2,1)S(1)}, u32[]{:S(2)}, u32[]{:S(2)}) collective-permute-start(bf16[48,1536]{1,0:T(8,128)(2,1)S(1)} %collective-permute-done.10), channel_id=1, source_target_pairs={{0,2},{2,4},{4,6},{6,0},{1,3},{3,5},{5,7},{7,1},{8,10},{10,12},{12... | collective-permute-start | bytes 442376 | tf_op jit(solution)/shard_map/ppermute | solution.py:393
  119.4 201.5 %collective-permute-start.37 = (bf16[128,1536]{1,0:T(8,128)(2,1)}, bf16[128,1536]{1,0:T(8,128)(2,1)}, u32[]{:S(2)}, u32[]{:S(2)}) collective-permute-start(bf16[128,1536]{1,0:T(8,128)(2,1)} %collective-permute-done.32), channel_id=1, source_target_pairs={{0,8},{8,0},{1,9},{9,1},{2,10},{10,2},{3,11},{11,3},{4,12},{12,4},... | collective-permute-start | bytes 1179656 | tf_op jit(solution)/shard_map/ppermute | solution.py:388
  120.1 191.2 %collective-permute-start.36 = (bf16[128,1536]{1,0:T(8,128)(2,1)}, bf16[128,1536]{1,0:T(8,128)(2,1)}, u32[]{:S(2)}, u32[]{:S(2)}) collective-permute-start(bf16[128,1536]{1,0:T(8,128)(2,1)} %collective-permute-done.31), channel_id=1, source_target_pairs={{0,8},{8,0},{1,9},{9,1},{2,10},{10,2},{3,11},{11,3},{4,12},{12,4},... | collective-permute-start | bytes 1179656 | tf_op jit(solution)/shard_map/ppermute | solution.py:388
  129.1 24.4 %collective-permute-start.5 = (bf16[128,1536]{1,0:T(8,128)(2,1)}, bf16[128,1536]{1,0:T(8,128)(2,1)}, u32[]{:S(2)}, u32[]{:S(2)}) collective-permute-start(bf16[128,1536]{1,0:T(8,128)(2,1)} %collective-permute-done.3), channel_id=1, source_target_pairs={{0,2},{2,4},{4,6},{6,0},{1,3},{3,5},{5,7},{7,1},{8,10},{10,12},{12... | collective-permute-start | bytes 1179656 | tf_op jit(solution)/shard_map/ppermute | solution.py:393
  150.9 22.7 %collective-permute-start.7 = (bf16[8,48,1152]{2,1,0:T(8,128)(2,1)}, bf16[8,48,1152]{2,1,0:T(8,128)(2,1)S(1)}, u32[]{:S(2)}, u32[]{:S(2)}) collective-permute-start(bf16[8,48,1152]{2,1,0:T(8,128)(2,1)} %all-to-all-done), channel_id=1, source_target_pairs={{0,16},{16,0},{1,17},{17,1},{2,18},{18,2},{3,19},{19,3},{4,20},{20... | collective-permute-start | bytes 2654216 | tf_op jit(solution)/shard_map/ppermute | solution.py:388
  153.5 42.6 %collective-permute-start.13 = (bf16[384,1536]{1,0:T(8,128)(2,1)}, bf16[384,1536]{1,0:T(8,128)(2,1)S(1)}, u32[]{:S(2)}, u32[]{:S(2)}) collective-permute-start(bf16[384,1536]{1,0:T(8,128)(2,1)} %bitcast.328), channel_id=1, source_target_pairs={{0,16},{16,0},{1,17},{17,1},{2,18},{18,2},{3,19},{19,3},{4,20},{20... | collective-permute-start | bytes 3538952 | tf_op jit(solution)/shard_map/ppermute | solution.py:388
  198.0 80.2 %collective-permute-start.14 = (bf16[768,1536]{1,0:T(8,128)(2,1)}, bf16[768,1536]{1,0:T(8,128)(2,1)}, u32[]{:S(2)}, u32[]{:S(2)}) collective-permute-start(bf16[768,1536]{1,0:T(8,128)(2,1)} %bitcast.41), channel_id=1, source_target_pairs={{0,8},{8,0},{1,9},{9,1},{2,10},{10,2},{3,11},{11,3},{4,12},{12,4},... | collective-permute-start | bytes 7077896 | tf_op jit(solution)/shard_map/ppermute | solution.py:388
  271.1 22.5 %all-to-all-start.1 = ((bf16[8,128,256]{1,2,0:T(8,128)(2,1)}), bf16[8,128,256]{1,2,0:T(8,128)(2,1)S(1)}, u32[]{:S(2)}, u32[]{:S(2)}) async-start(bf16[8,128,256]{1,2,0:T(8,128)(2,1)} %copy.103), calls=%async_computation.1 | async-start | bytes 1048576 | tf_op jit(solution)/shard_map/all_to_all | solution.py:384
  277.9 317.3 %reduce-scatter.5.cloned.1.call-start = ((), (), s32[]{:S(2)}) async-start(), calls=%async_computation.11 | async-start | bytes 1966080 | tf_op jit(solution)/shard_map/reduce_scatter | solution.py:380
  300.8 22.6 %collective-permute-start.38 = (bf16[128,1536]{1,0:T(8,128)(2,1)}, bf16[128,1536]{1,0:T(8,128)(2,1)S(1)}, u32[]{:S(2)}, u32[]{:S(2)}) collective-permute-start(bf16[128,1536]{1,0:T(8,128)(2,1)} %pad_maximum_fusion.11), channel_id=1, source_target_pairs={{0,8},{8,0},{1,9},{9,1},{2,10},{10,2},{3,11},{11,3},{4,12},{12,4},... | collective-permute-start | bytes 1179656 | tf_op jit(solution)/shard_map/ppermute | solution.py:388
  350.4 324.4 %reduce-scatter.3.cloned.1.call-start = ((), (), s32[]{:S(2)}) async-start(), calls=%async_computation.10 | async-start | bytes 3932160 | tf_op jit(solution)/shard_map/reduce_scatter | solution.py:380
  364.7 34.5 %collective-permute-start.39 = (bf16[128,1536]{1,0:T(8,128)(2,1)S(1)}, bf16[128,1536]{1,0:T(8,128)(2,1)}, u32[]{:S(2)}, u32[]{:S(2)}) collective-permute-start(bf16[128,1536]{1,0:T(8,128)(2,1)S(1)} %get-tuple-element.77), channel_id=1, source_target_pairs={{0,8},{8,0},{1,9},{9,1},{2,10},{10,2},{3,11},{11,3},{4,12},{12,4},... | collective-permute-start | bytes 1179656 | tf_op jit(solution)/shard_map/ppermute | solution.py:388
  371.3 39.2 %collective-permute-start.23 = (bf16[128,1536]{1,0:T(8,128)(2,1)}, bf16[128,1536]{1,0:T(8,128)(2,1)S(1)}, u32[]{:S(2)}, u32[]{:S(2)}) collective-permute-start(bf16[128,1536]{1,0:T(8,128)(2,1)} %get-tuple-element.81), channel_id=1, source_target_pairs={{0,8},{8,0},{1,9},{9,1},{2,10},{10,2},{3,11},{11,3},{4,12},{12,4},... | collective-permute-start | bytes 1179656 | tf_op jit(solution)/shard_map/ppermute | solution.py:388
  421.8 32.3 %all-to-all-start.3 = ((bf16[8,128,256]{1,2,0:T(8,128)(2,1)}), bf16[8,128,256]{1,2,0:T(8,128)(2,1)S(1)}, u32[]{:S(2)}, u32[]{:S(2)}) async-start(bf16[8,128,256]{1,2,0:T(8,128)(2,1)} %bitcast.80), calls=%async_computation.3 | async-start | bytes 1048576 | tf_op jit(solution)/shard_map/all_to_all | solution.py:384
  432.3 153.8 %collective-permute-start.56 = (bf16[768,1536]{1,0:T(8,128)(2,1)}, bf16[768,1536]{1,0:T(8,128)(2,1)}, u32[]{:S(2)}, u32[]{:S(2)}) collective-permute-start(bf16[768,1536]{1,0:T(8,128)(2,1)} %select_convert_fusion), channel_id=1, source_target_pairs={{0,8},{8,0},{1,9},{9,1},{2,10},{10,2},{3,11},{11,3},{4,12},{12,4},... | collective-permute-start | bytes 7077896 | tf_op jit(solution)/shard_map/ppermute | solution.py:388
  526.9 70.3 %collective-permute-start.47 = (bf16[128,1536]{1,0:T(8,128)(2,1)}, bf16[128,1536]{1,0:T(8,128)(2,1)S(1)}, u32[]{:S(2)}, u32[]{:S(2)}) collective-permute-start(bf16[128,1536]{1,0:T(8,128)(2,1)} %get-tuple-element.58), channel_id=1, source_target_pairs={{0,1},{1,0},{2,3},{3,2},{4,5},{5,4},{6,7},{7,6},{8,9},{9,8},{10,11... | collective-permute-start | bytes 1179656 | tf_op jit(solution)/shard_map/ppermute | solution.py:388
  528.0 19.6 %collective-permute-start.50 = (bf16[128,1536]{1,0:T(8,128)(2,1)S(1)}, bf16[128,1536]{1,0:T(8,128)(2,1)S(1)}, u32[]{:S(2)}, u32[]{:S(2)}) collective-permute-start(bf16[128,1536]{1,0:T(8,128)(2,1)S(1)} %get-tuple-element.59), channel_id=1, source_target_pairs={{0,1},{1,0},{2,3},{3,2},{4,5},{5,4},{6,7},{7,6},{8,9},{9,8},{10,11... | collective-permute-start | bytes 1179656 | tf_op jit(solution)/shard_map/ppermute | solution.py:388
  529.0 44.5 %collective-permute-start.49 = (bf16[128,1536]{1,0:T(8,128)(2,1)S(1)}, bf16[128,1536]{1,0:T(8,128)(2,1)S(1)}, u32[]{:S(2)}, u32[]{:S(2)}) collective-permute-start(bf16[128,1536]{1,0:T(8,128)(2,1)S(1)} %get-tuple-element.60), channel_id=1, source_target_pairs={{0,1},{1,0},{2,3},{3,2},{4,5},{5,4},{6,7},{7,6},{8,9},{9,8},{10,11... | collective-permute-start | bytes 1179656 | tf_op jit(solution)/shard_map/ppermute | solution.py:388
  530.0 49.8 %collective-permute-start.48 = (bf16[128,1536]{1,0:T(8,128)(2,1)S(1)}, bf16[128,1536]{1,0:T(8,128)(2,1)}, u32[]{:S(2)}, u32[]{:S(2)}) collective-permute-start(bf16[128,1536]{1,0:T(8,128)(2,1)S(1)} %get-tuple-element.61), channel_id=1, source_target_pairs={{0,1},{1,0},{2,3},{3,2},{4,5},{5,4},{6,7},{7,6},{8,9},{9,8},{10,11... | collective-permute-start | bytes 1179656 | tf_op jit(solution)/shard_map/ppermute | solution.py:388
  548.4 25.1 %collective-permute-start.51 = (bf16[128,1536]{1,0:T(8,128)(2,1)}, bf16[128,1536]{1,0:T(8,128)(2,1)S(1)}, u32[]{:S(2)}, u32[]{:S(2)}) collective-permute-start(bf16[128,1536]{1,0:T(8,128)(2,1)} %fusion.31), channel_id=1, source_target_pairs={{0,2},{2,4},{4,6},{6,0},{1,3},{3,5},{5,7},{7,1},{8,10},{10,12},{12... | collective-permute-start | bytes 1179656 | tf_op jit(solution)/shard_map/ppermute | solution.py:393
  595.3 26.0 %collective-permute-start.57 = (bf16[384,1536]{1,0:T(8,128)(2,1)}, bf16[384,1536]{1,0:T(8,128)(2,1)}, u32[]{:S(2)}, u32[]{:S(2)}) collective-permute-start(bf16[384,1536]{1,0:T(8,128)(2,1)} %select_convert_fusion.2), channel_id=1, source_target_pairs={{0,16},{16,0},{1,17},{17,1},{2,18},{18,2},{3,19},{19,3},{4,20},{20... | collective-permute-start | bytes 3538952 | tf_op jit(solution)/shard_map/ppermute | solution.py:388
  644.5 30.2 %all-to-all-start.4 = ((bf16[8,48,1152]{2,1,0:T(8,128)(2,1)}), bf16[8,48,1152]{2,1,0:T(8,128)(2,1)S(1)}, u32[]{:S(2)}, u32[]{:S(2)}) async-start(bf16[8,48,1152]{2,1,0:T(8,128)(2,1)} %bitcast.339), calls=%async_computation.4 | async-start | bytes 1769472 | tf_op jit(solution)/shard_map/all_to_all | solution.py:384
  649.8 19.5 %collective-permute-start.60 = (bf16[48,1536]{1,0:T(8,128)(2,1)S(1)}, bf16[48,1536]{1,0:T(8,128)(2,1)S(1)}, u32[]{:S(2)}, u32[]{:S(2)}) collective-permute-start(bf16[48,1536]{1,0:T(8,128)(2,1)S(1)} %fusion.47), channel_id=1, source_target_pairs={{0,2},{2,4},{4,6},{6,0},{1,3},{3,5},{5,7},{7,1},{8,10},{10,12},{12... | collective-permute-start | bytes 442376 | tf_op jit(solution)/shard_map/ppermute | solution.py:393
  (88 other events, 1003.1 us)
Sparse Core Ops, SparseCore 0:
  27.4 101.4 all-gather.2
  130.4 35.0 all-gather.4
  350.5 33.6 reduce-scatter.4
  386.3 67.5 reduce-scatter.2

commit v3 on v2

--- a/solution.py
+++ b/solution.py
@@ -482,6 +482,19 @@
     return total
 
 
+def unpack_kernel(n, cols, recv_ref, *outs):
+    for i, out in enumerate(outs):
+        for s in range(n):
+            out[:, s * cols:(s + 1) * cols] = recv_ref[s, :, i * cols:(i + 1) * cols].astype(f32)
+
+
+def unpack(recv, cols, width):
+    return pl.pallas_call(functools.partial(unpack_kernel, width // cols, cols),
+        out_shape=[jax.ShapeDtypeStruct((recv.shape[1], width), f32)] * 4,
+        cost_estimate=spent(3),
+    )(recv)
+
+
 def on_device(inputs, doc_lengths, w_query, w_key, w_value, w_house, w_beta, beta_bias, norm_attn, w_out,
               norm_mlp, w_gate, w_up, w_down, grad_y):
     hi_n, lo_n = lax.axis_size("hi"), lax.axis_size("lo")
@@ -611,13 +624,13 @@
     grad_pack = jnp.concatenate([grad_pack[:, :4 * head_cols], spare_grad], axis=1)
     grad_pack = jnp.swapaxes(grad_pack.reshape(dp_n // 2, 2, -1, slot), 0, 1)
     grad_pack = keep(keep(grad_pack, "core"), "x").astype(bf16)
-    grad_pack = exchange(grad_pack.reshape(seq_n, rows, slot), SEQ).astype(f32)
+    grad_pack = exchange(grad_pack.reshape(seq_n, rows, slot), SEQ)
 
     def whole(part, n):
         return jnp.swapaxes(part, 0, 1).reshape(rows, -1)[:, :n]
 
-    grads = [whole(grad_pack[:, :, i * head_cols:(i + 1) * head_cols], width) for i in range(4)]
-    spare_grad = grad_pack[:, :, 4 * head_cols:]
+    grads = unpack(grad_pack, head_cols, width)
+    spare_grad = grad_pack[:, :, 4 * head_cols:].astype(f32)
     grad_beta = whole(spare_grad[:, :, :nh], HEADS)
     grad_gain_attn = jnp.sum(spare_grad[:, :, nh:nh + dp_n], axis=(0, 2))
     grad_gain_mlp = jnp.sum(spare_grad[:, :, nh + dp_n:base], axis=(0, 2))

time: 712 us -> 701 us (0.985)
  local copies, waits for them, and re-layouts: 97.9 us -> 88 us
    all_to_all x5, waiting for transfers between devices: 37.6 us -> 19.9 us  [exchange(): return lax.all_to_all(pieces, axes, 0, 0, tiled=True)]
    ppermute x12, waiting for transfers between devices: 49.6 us -> 65.2 us  [ring(): return lax.ppermute(a, 'hi', [(i, (i + 1) % n) for i in range(n)])]
    ppermute x50, starting transfers between devices: 33.3 us -> 41.4 us  [swap(): return lax.ppermute(a, axis, [(0, 1), (1, 0)])]
    unnamed x111 -> x110, local copies, waits for them, and re-layouts: 23.7 us -> 18.1 us
  transfers between devices with their start and end apart: 71 -> 71, of which waited for: 27 -> 29; matrix products, arithmetic and copies ran while one was open for 28% -> 26% of each run, Pallas kernels for 17% -> 18%
where the time goes in v3:
time: 701 us; the launch traced here: 694 us
  waiting for transfers between devices  220 us (31%)
  Pallas kernels  122 us (17%)
  starting transfers between devices  109 us (16%)
  local copies, waits for them, and re-layouts  88 us (13%)
  other arithmetic  62.2 us (9%)
  matrix products  58.4 us (8%)
  between operations  17.9 us (3%)
  blocking collectives  16.7 us (2%)
    ppermute x50, waiting for transfers between devices, swap(): return lax.ppermute(a, axis, [(0, 1), (1, 0)])  134 us
    ppermute x12, waiting for transfers between devices, ring(): return lax.ppermute(a, 'hi', [(i, (i + 1) % n) for i in range(n)])  65.2 us
    ppermute x12, starting transfers between devices, ring(): return lax.ppermute(a, 'hi', [(i, (i + 1) % n) for i in range(n)])  43.7 us
    ppermute x50, starting transfers between devices, swap(): return lax.ppermute(a, axis, [(0, 1), (1, 0)])  41.4 us
    pallas_call x1, Pallas kernels, run_factors(): pl.pallas_call(functools.partial(factor_kernel, nh), grid=(L // PAIR,), i...  40.6 us
    pallas_call x1, Pallas kernels, run_factor_back(): pl.pallas_call(functools.partial(factor_back_kernel, nh), grid=(L // PAIR...  30.2 us
    pallas_call x1, Pallas kernels, run_backward(): pl.pallas_call(functools.partial(backward_kernel, nh, docs, G), grid=(G,)...  29.6 us
    dot_general x4, matrix products, dot_nt(): lax.dot_general(a, b, (((1,), (1,)), ((), ())), preferred_element_type=f32)  24.9 us
  transfers between devices with their start and end apart: 71, of which 29 were waited for; matrix products, arithmetic and copies ran while one was open for 26% of the time, Pallas kernels for 18%

profile of v3, /device:TPU:0, one launch (start us, length us, event | category | flops | bytes accessed | tf_op | source)
XLA Modules:
  0.0 694.3 jit_solution(14993611300828535831)
XLA Ops:
  10.5 16.7 %all_to_all.30 = bf16[8,48,1024]{2,1,0:T(8,128)(2,1)} all-to-all(bf16[8,48,1024]{2,1,0:T(8,128)(2,1)S(1)} %pad_maximum_fusion.7), channel_id=1, replica_groups=mesh['x'=2,'core'=2,'hi'=4,'lo'=2] {'x','core','lo'}, dimensions={0} | all-to-all | bytes 1572864 | tf_op jit(solution)/shard_map/all_to_all | solution.py:384
  51.5 9.7 %collective-permute-start.10 = (bf16[48,1536]{1,0:T(8,128)(2,1)}, bf16[48,1536]{1,0:T(8,128)(2,1)S(1)}, u32[]{:S(2)}, u32[]{:S(2)}) collective-permute-start(bf16[48,1536]{1,0:T(8,128)(2,1)} %collective-permute-done.9), channel_id=1, source_target_pairs={{0,2},{2,4},{4,6},{6,0},{1,3},{3,5},{5,7},{7,1},{8,10},{10,12},{12... | collective-permute-start | bytes 442376 | tf_op jit(solution)/shard_map/ppermute | solution.py:393
  62.8 21.7 %collective-permute-done.10 = bf16[48,1536]{1,0:T(8,128)(2,1)S(1)} collective-permute-done((bf16[48,1536]{1,0:T(8,128)(2,1)}, bf16[48,1536]{1,0:T(8,128)(2,1)S(1)}, u32[]{:S(2)}, u32[]{:S(2)}) %collective-permute-start.10) | collective-permute-done | bytes 147488 | tf_op jit(solution)/shard_map/ppermute | solution.py:393
  85.2 20.7 %collective-permute-start.11 = (bf16[48,1536]{1,0:T(8,128)(2,1)S(1)}, bf16[48,1536]{1,0:T(8,128)(2,1)S(1)}, u32[]{:S(2)}, u32[]{:S(2)}) collective-permute-start(bf16[48,1536]{1,0:T(8,128)(2,1)S(1)} %collective-permute-done.10), channel_id=1, source_target_pairs={{0,2},{2,4},{4,6},{6,0},{1,3},{3,5},{5,7},{7,1},{8,10},{10,12},{12... | collective-permute-start | bytes 442376 | tf_op jit(solution)/shard_map/ppermute | solution.py:393
  130.7 9.8 %collective-permute-done.12 = bf16[192,1536]{1,0:T(8,128)(2,1)S(1)} collective-permute-done((bf16[192,1536]{1,0:T(8,128)(2,1)}, bf16[192,1536]{1,0:T(8,128)(2,1)S(1)}, u32[]{:S(2)}, u32[]{:S(2)}) %collective-permute-start.12) | collective-permute-done | bytes 589856 | tf_op jit(solution)/shard_map/ppermute | solution.py:388
  144.5 6.4 collective-permute-done.4
  155.1 18.6 %collective-permute-done.7 = bf16[8,48,1152]{2,1,0:T(8,128)(2,1)S(1)} collective-permute-done((bf16[8,48,1152]{2,1,0:T(8,128)(2,1)}, bf16[8,48,1152]{2,1,0:T(8,128)(2,1)S(1)}, u32[]{:S(2)}, u32[]{:S(2)}) %collective-permute-start.7) | collective-permute-done | bytes 884768 | tf_op jit(solution)/shard_map/ppermute | solution.py:388
  182.4 13.8 %collective-permute-done.13 = bf16[384,1536]{1,0:T(8,128)(2,1)S(1)} collective-permute-done((bf16[384,1536]{1,0:T(8,128)(2,1)}, bf16[384,1536]{1,0:T(8,128)(2,1)S(1)}, u32[]{:S(2)}, u32[]{:S(2)}) %collective-permute-start.13) | collective-permute-done | bytes 1179680 | tf_op jit(solution)/shard_map/ppermute | solution.py:388
  200.6 5.8 fusion.58.proj_ref
  206.4 40.6 %shard_map.254 = (bf16[2,1024,128]{2,1,0:T(8,128)(2,1)}, bf16[2,1024,128]{2,1,0:T(8,128)(2,1)}, bf16[2,1024,128]{2,1,0:T(8,128)(2,1)}, bf16[2,1024,128]{2,1,0:T(...) custom-call(f32[1024,1152]{1,0:T(8,128)} %fusion.58.proj_ref, ...), custom_call_target="tpu_custom_call" | custom-call | flops 41799999488 | bytes 1048576 | tf_op jit(solution)/shard_map/pallas_call | solution.py:90
  249.5 19.4 %shard_map.255 = (bf16[1024,256]{1,0:T(8,128)(2,1)}, f32[2,1024,128]{2,1,0:T(8,128)}, bf16[8,2,2,1024,128]{4,3,2,1,0:T(8,128)(2,1)}) custom-call(s32[4]{0:T(128)} %bitcast.363, bf16[2,1024,128]{2,1,0:T(8,128)(2,1)} %get-tuple-element.36.qm_ref, bf16[2,1024,128]{2,1,0:T(8,128)(2,1)} %get-tuple-element.37.kmf_ref, ...), custom_call_target="tpu_custom_call" | custom-call | flops 24199999488 | bytes 1048576 | tf_op jit(solution)/shard_map/pallas_call | solution.py:180
  271.0 6.8 all-to-all-start.1
  283.3 8.2 %all-to-all-done.1 = bf16[8,128,256]{1,2,0:T(8,128)(2,1)S(1)} async-done(((bf16[8,128,256]{1,2,0:T(8,128)(2,1)}), bf16[8,128,256]{1,2,0:T(8,128)(2,1)S(1)}, u32[]{:S(2)}, u32[]{:S(2)}) %all-to-all-start.1) | async-done | bytes 524320 | tf_op jit(solution)/shard_map/all_to_all | solution.py:384
  312.2 7.4 %collective-permute-done.18 = bf16[64,1536]{0,1:T(8,128)(2,1)S(1)} collective-permute-done((bf16[64,1536]{0,1:T(8,128)(2,1)S(1)}, bf16[64,1536]{0,1:T(8,128)(2,1)S(1)}, u32[]{:S(2)}, u32[]{:S(2)}) %collective-permute-start.18) | collective-permute-done | bytes 196640 | tf_op jit(solution)/shard_map/ppermute | solution.py:388
  324.9 6.5 concatenate.44
  331.4 8.3 %fusion.59 = f32[1024,1024]{0,1:T(8,128)} fusion(bf16[1024,1536]{0,1:T(8,128)(2,1)} %concatenate.44, bf16[1536,1024]{1,0:T(8,128)(2,1)} %bitcast.358), kind=kOutput, calls=%fused_computation.198 | convolution fusion | flops 3221225472 | bytes 10485760 | tf_op jit(solution)/shard_map/dot_general | solution.py:364
  339.7 7.5 %multiply_convert_fusion.3 = (bf16[1024,512]{0,1:T(8,128)(2,1)}, bf16[1024,512]{0,1:T(8,128)(2,1)}, bf16[1024,512]{0,1:T(8,128)(2,1)S(1)}) fusion(f32[1024,1024]{0,1:T(8,128)} %fusion.59, bf16[1024,1536]{1,0:T(8,128)(2,1)} %constant_dynamic-update-slice_fusion, bf16[512,1536]{1,0:T(8,128)(2,1)} %all-gather.5.cloned.1.call-done), kind=kOutput, calls=%fused_computation.23 | convolution fusion | flops 1618477056 | bytes 12058624 | tf_op jit(solution)/shard_map/dot_general | solution.py:368
  354.9 6.0 fusion.57
  420.0 5.4 all-to-all-done.3
  426.4 29.6 %shard_map.256 = (f32[2,1024,128]{2,1,0:T(8,128)}, bf16[2,1024,128]{2,1,0:T(8,128)(2,1)}, f32[2,1024,128]{2,1,0:T(8,128)}, f32[2,1024,128]{2,1,0:T(8,128)}, f32[...) custom-call(s32[4]{0:T(128)} %bitcast.364, bf16[2,1024,128]{2,1,0:T(8,128)(2,1)} %get-tuple-element.36.qm_ref, ...), custom_call_target="tpu_custom_call" | custom-call | flops 38499999744 | bytes 1048576 | tf_op jit(solution)/shard_map/pallas_call | solution.py:268
  456.1 30.2 %shard_map.257 = (bf16[1024,1152]{1,0:T(8,128)(2,1)}, f32[1,128]{1,0:T(1,128)}) custom-call(f32[1024,1152]{1,0:T(8,128)} %fusion.58.proj_ref, f32[2]{0:T(128)} %pad_dynamic-slice_fusion.bias_ref, bf16[2,1024,128]{2,1,0:T(8,128)(2,1)} %get-tuple-element.38.w_ref, bf16[2,1024,128]{2,1,0:T(8,128)(2,1)} %get-tuple-element.36.qm_ref, ...), custom_call_target="tpu_custom_call" | custom-call | flops 32999999488 | bytes 1048576 | tf_op jit(solution)/shard_map/pallas_call | solution.py:335
  490.2 7.1 %multiply_reduce_fusion = (f32[1536]{0:T(1024)S(1)}, bf16[1024,1536]{1,0:T(8,128)(2,1)S(1)}, f32[1024,1536]{1,0:T(8,128)S(1)}) fusion(bf16[4,2,128,1536]{3,2,1,0:T(8,128)(2,1)S(1)} %copy-done.3, f32[1024]{0:T(1024)S(1)} %bitcast.355, f32[1536]{0:T(1024)S(1)} %copy-done.27, bf16[1024,1152]{1,0:T(8,128)(2,1)} %get-tuple-element.52, ...), kind=kOutput, calls=%fused_computation.2 | convolution fusion | flops 3633314304 | bytes 18497536 | tf_op jit(solution)/shard_map/dot_general | solution.py:368
  507.4 11.5 %collective-permute-done.50 = bf16[128,1536]{1,0:T(8,128)(2,1)S(1)} collective-permute-done((bf16[128,1536]{1,0:T(8,128)(2,1)S(1)}, bf16[128,1536]{1,0:T(8,128)(2,1)S(1)}, u32[]{:S(2)}, u32[]{:S(2)}) %collective-permute-start.50) | collective-permute-done | bytes 393248 | tf_op jit(solution)/shard_map/ppermute | solution.py:388
  523.9 9.4 %reshape.361 = f32[2,2,384,1152]{2,1,0,3:T(2,128)} reshape(f32[1536,1152]{0,1:T(8,128)} %pad_maximum_fusion) | data formatting | bytes 14155776 | tf_op jit(solution)/shard_map/reshape | solution.py:625
  533.3 12.3 %copy.103 = f32[2,2,384,1152]{3,2,0,1:T(8,128)} copy(f32[2,2,384,1152]{2,1,0,3:T(2,128)} %reshape.361) | data formatting | bytes 14155776 | tf_op jit(solution)/shard_map/reshape | solution.py:625
  558.2 5.8 convert_add_fusion
  568.8 5.9 convolution_convert_fusion
  582.0 13.5 %collective-permute-done.57 = bf16[384,1536]{1,0:T(8,128)(2,1)} collective-permute-done((bf16[384,1536]{1,0:T(8,128)(2,1)}, bf16[384,1536]{1,0:T(8,128)(2,1)}, u32[]{:S(2)}, u32[]{:S(2)}) %collective-permute-start.57) | collective-permute-done | bytes 1179680 | tf_op jit(solution)/shard_map/ppermute | solution.py:388
  601.2 11.2 %collective-permute-done.58 = bf16[192,1536]{1,0:T(8,128)(2,1)S(1)} collective-permute-done((bf16[192,1536]{1,0:T(8,128)(2,1)S(1)}, bf16[192,1536]{1,0:T(8,128)(2,1)S(1)}, u32[]{:S(2)}, u32[]{:S(2)}) %collective-permute-start.58) | collective-permute-done | bytes 589856 | tf_op jit(solution)/shard_map/ppermute | solution.py:388
  613.6 6.8 collective-permute-done.55
  627.9 30.6 %collective-permute-done.60 = bf16[48,1536]{1,0:T(8,128)(2,1)S(1)} collective-permute-done((bf16[48,1536]{1,0:T(8,128)(2,1)S(1)}, bf16[48,1536]{1,0:T(8,128)(2,1)S(1)}, u32[]{:S(2)}, u32[]{:S(2)}) %collective-permute-start.60) | collective-permute-done | bytes 147488 | tf_op jit(solution)/shard_map/ppermute | solution.py:393
  675.8 6.2 all-to-all-done.5
  (388 shorter events, 257.1 us)
Async XLA Ops:
  7.2 324.2 %all-gather.3.cloned.1.call-start = ((), (), s32[]{:S(2)}) async-start(), calls=%async_computation.8 | async-start | bytes 3932160 | tf_op jit(solution)/shard_map/all_gather | solution.py:376
  27.3 82.6 %collective-permute-start = (bf16[128,1536]{1,0:T(8,128)(2,1)S(1)}, bf16[128,1536]{1,0:T(8,128)(2,1)}, u32[]{:S(2)}, u32[]{:S(2)}) collective-permute-start(bf16[128,1536]{1,0:T(8,128)(2,1)S(1)} %bitcast.304), channel_id=1, source_target_pairs={{0,1},{1,0},{2,3},{3,2},{4,5},{5,4},{6,7},{7,6},{8,9},{9,8},{10,11... | collective-permute-start | bytes 1179656 | tf_op jit(solution)/shard_map/ppermute | solution.py:388
  28.8 81.8 %collective-permute-start.1 = (bf16[128,1536]{1,0:T(8,128)(2,1)S(1)}, bf16[128,1536]{1,0:T(8,128)(2,1)}, u32[]{:S(2)}, u32[]{:S(2)}) collective-permute-start(bf16[128,1536]{1,0:T(8,128)(2,1)S(1)} %bitcast.305), channel_id=1, source_target_pairs={{0,2},{2,4},{4,6},{6,0},{1,3},{3,5},{5,7},{7,1},{8,10},{10,12},{12... | collective-permute-start | bytes 1179656 | tf_op jit(solution)/shard_map/ppermute | solution.py:393
  30.4 54.7 %collective-permute-start.32 = (bf16[128,1536]{1,0:T(8,128)(2,1)}, bf16[128,1536]{1,0:T(8,128)(2,1)}, u32[]{:S(2)}, u32[]{:S(2)}) collective-permute-start(bf16[128,1536]{1,0:T(8,128)(2,1)} %bitcast.61), channel_id=1, source_target_pairs={{0,16},{16,0},{1,17},{17,1},{2,18},{18,2},{3,19},{19,3},{4,20},{20... | collective-permute-start | bytes 1179656 | tf_op jit(solution)/shard_map/ppermute | solution.py:388
  31.0 75.8 %collective-permute-start.31 = (bf16[128,1536]{1,0:T(8,128)(2,1)}, bf16[128,1536]{1,0:T(8,128)(2,1)}, u32[]{:S(2)}, u32[]{:S(2)}) collective-permute-start(bf16[128,1536]{1,0:T(8,128)(2,1)} %bitcast.61), channel_id=1, source_target_pairs={{0,1},{1,0},{2,3},{3,2},{4,5},{5,4},{6,7},{7,6},{8,9},{9,8},{10,11... | collective-permute-start | bytes 1179656 | tf_op jit(solution)/shard_map/ppermute | solution.py:388
  35.8 115.1 %all-to-all-start = ((bf16[8,48,1152]{2,1,0:T(8,128)(2,1)}), bf16[8,48,1152]{2,1,0:T(8,128)(2,1)}, u32[]{:S(2)}, u32[]{:S(2)}) async-start(bf16[8,48,1152]{2,1,0:T(8,128)(2,1)} %copy.85), calls=%async_computation | async-start | bytes 1769472 | tf_op jit(solution)/shard_map/all_to_all | solution.py:384
  40.1 299.6 %all-gather.5.cloned.1.call-start = ((), (), s32[]{:S(2)}) async-start(), calls=%async_computation.9 | async-start | bytes 1966080 | tf_op jit(solution)/shard_map/all_gather | solution.py:376
  51.5 33.0 %collective-permute-start.10 = (bf16[48,1536]{1,0:T(8,128)(2,1)}, bf16[48,1536]{1,0:T(8,128)(2,1)S(1)}, u32[]{:S(2)}, u32[]{:S(2)}) collective-permute-start(bf16[48,1536]{1,0:T(8,128)(2,1)} %collective-permute-done.9), channel_id=1, source_target_pairs={{0,2},{2,4},{4,6},{6,0},{1,3},{3,5},{5,7},{7,1},{8,10},{10,12},{12... | collective-permute-start | bytes 442376 | tf_op jit(solution)/shard_map/ppermute | solution.py:393
  84.5 214.2 %collective-permute-start.35 = (bf16[128,1536]{1,0:T(8,128)(2,1)}, bf16[128,1536]{1,0:T(8,128)(2,1)}, u32[]{:S(2)}, u32[]{:S(2)}) collective-permute-start(bf16[128,1536]{1,0:T(8,128)(2,1)} %bitcast.61), channel_id=1, source_target_pairs={{0,8},{8,0},{1,9},{9,1},{2,10},{10,2},{3,11},{11,3},{4,12},{12,4},... | collective-permute-start | bytes 1179656 | tf_op jit(solution)/shard_map/ppermute | solution.py:388
  85.2 32.0 %collective-permute-start.11 = (bf16[48,1536]{1,0:T(8,128)(2,1)S(1)}, bf16[48,1536]{1,0:T(8,128)(2,1)S(1)}, u32[]{:S(2)}, u32[]{:S(2)}) collective-permute-start(bf16[48,1536]{1,0:T(8,128)(2,1)S(1)} %collective-permute-done.10), channel_id=1, source_target_pairs={{0,2},{2,4},{4,6},{6,0},{1,3},{3,5},{5,7},{7,1},{8,10},{10,12},{12... | collective-permute-start | bytes 442376 | tf_op jit(solution)/shard_map/ppermute | solution.py:393
  119.4 201.6 %collective-permute-start.37 = (bf16[128,1536]{1,0:T(8,128)(2,1)}, bf16[128,1536]{1,0:T(8,128)(2,1)}, u32[]{:S(2)}, u32[]{:S(2)}) collective-permute-start(bf16[128,1536]{1,0:T(8,128)(2,1)} %collective-permute-done.32), channel_id=1, source_target_pairs={{0,8},{8,0},{1,9},{9,1},{2,10},{10,2},{3,11},{11,3},{4,12},{12,4},... | collective-permute-start | bytes 1179656 | tf_op jit(solution)/shard_map/ppermute | solution.py:388
  120.1 190.4 %collective-permute-start.36 = (bf16[128,1536]{1,0:T(8,128)(2,1)}, bf16[128,1536]{1,0:T(8,128)(2,1)}, u32[]{:S(2)}, u32[]{:S(2)}) collective-permute-start(bf16[128,1536]{1,0:T(8,128)(2,1)} %collective-permute-done.31), channel_id=1, source_target_pairs={{0,8},{8,0},{1,9},{9,1},{2,10},{10,2},{3,11},{11,3},{4,12},{12,4},... | collective-permute-start | bytes 1179656 | tf_op jit(solution)/shard_map/ppermute | solution.py:388
  129.1 24.5 %collective-permute-start.5 = (bf16[128,1536]{1,0:T(8,128)(2,1)}, bf16[128,1536]{1,0:T(8,128)(2,1)}, u32[]{:S(2)}, u32[]{:S(2)}) collective-permute-start(bf16[128,1536]{1,0:T(8,128)(2,1)} %collective-permute-done.3), channel_id=1, source_target_pairs={{0,2},{2,4},{4,6},{6,0},{1,3},{3,5},{5,7},{7,1},{8,10},{10,12},{12... | collective-permute-start | bytes 1179656 | tf_op jit(solution)/shard_map/ppermute | solution.py:393
  150.9 22.7 %collective-permute-start.7 = (bf16[8,48,1152]{2,1,0:T(8,128)(2,1)}, bf16[8,48,1152]{2,1,0:T(8,128)(2,1)S(1)}, u32[]{:S(2)}, u32[]{:S(2)}) collective-permute-start(bf16[8,48,1152]{2,1,0:T(8,128)(2,1)} %all-to-all-done), channel_id=1, source_target_pairs={{0,16},{16,0},{1,17},{17,1},{2,18},{18,2},{3,19},{19,3},{4,20},{20... | collective-permute-start | bytes 2654216 | tf_op jit(solution)/shard_map/ppermute | solution.py:388
  153.5 42.6 %collective-permute-start.13 = (bf16[384,1536]{1,0:T(8,128)(2,1)}, bf16[384,1536]{1,0:T(8,128)(2,1)S(1)}, u32[]{:S(2)}, u32[]{:S(2)}) collective-permute-start(bf16[384,1536]{1,0:T(8,128)(2,1)} %bitcast.312), channel_id=1, source_target_pairs={{0,16},{16,0},{1,17},{17,1},{2,18},{18,2},{3,19},{19,3},{4,20},{20... | collective-permute-start | bytes 3538952 | tf_op jit(solution)/shard_map/ppermute | solution.py:388
  198.0 80.0 %collective-permute-start.14 = (bf16[768,1536]{1,0:T(8,128)(2,1)}, bf16[768,1536]{1,0:T(8,128)(2,1)}, u32[]{:S(2)}, u32[]{:S(2)}) collective-permute-start(bf16[768,1536]{1,0:T(8,128)(2,1)} %bitcast.41), channel_id=1, source_target_pairs={{0,8},{8,0},{1,9},{9,1},{2,10},{10,2},{3,11},{11,3},{4,12},{12,4},... | collective-permute-start | bytes 7077896 | tf_op jit(solution)/shard_map/ppermute | solution.py:388
  271.0 20.5 %all-to-all-start.1 = ((bf16[8,128,256]{1,2,0:T(8,128)(2,1)}), bf16[8,128,256]{1,2,0:T(8,128)(2,1)S(1)}, u32[]{:S(2)}, u32[]{:S(2)}) async-start(bf16[8,128,256]{1,2,0:T(8,128)(2,1)} %copy.89), calls=%async_computation.1 | async-start | bytes 1048576 | tf_op jit(solution)/shard_map/all_to_all | solution.py:384
  277.8 296.9 %reduce-scatter.5.cloned.1.call-start = ((), (), s32[]{:S(2)}) async-start(), calls=%async_computation.11 | async-start | bytes 1966080 | tf_op jit(solution)/shard_map/reduce_scatter | solution.py:380
  298.7 24.6 %collective-permute-start.38 = (bf16[128,1536]{1,0:T(8,128)(2,1)}, bf16[128,1536]{1,0:T(8,128)(2,1)S(1)}, u32[]{:S(2)}, u32[]{:S(2)}) collective-permute-start(bf16[128,1536]{1,0:T(8,128)(2,1)} %pad_maximum_fusion.11), channel_id=1, source_target_pairs={{0,8},{8,0},{1,9},{9,1},{2,10},{10,2},{3,11},{11,3},{4,12},{12,4},... | collective-permute-start | bytes 1179656 | tf_op jit(solution)/shard_map/ppermute | solution.py:388
  361.1 25.2 %collective-permute-start.39 = (bf16[128,1536]{1,0:T(8,128)(2,1)S(1)}, bf16[128,1536]{1,0:T(8,128)(2,1)S(1)}, u32[]{:S(2)}, u32[]{:S(2)}) collective-permute-start(bf16[128,1536]{1,0:T(8,128)(2,1)S(1)} %get-tuple-element.85), channel_id=1, source_target_pairs={{0,8},{8,0},{1,9},{9,1},{2,10},{10,2},{3,11},{11,3},{4,12},{12,4},... | collective-permute-start | bytes 1179656 | tf_op jit(solution)/shard_map/ppermute | solution.py:388
  366.2 29.7 %collective-permute-start.23 = (bf16[128,1536]{1,0:T(8,128)(2,1)}, bf16[128,1536]{1,0:T(8,128)(2,1)S(1)}, u32[]{:S(2)}, u32[]{:S(2)}) collective-permute-start(bf16[128,1536]{1,0:T(8,128)(2,1)} %get-tuple-element.89), channel_id=1, source_target_pairs={{0,8},{8,0},{1,9},{9,1},{2,10},{10,2},{3,11},{11,3},{4,12},{12,4},... | collective-permute-start | bytes 1179656 | tf_op jit(solution)/shard_map/ppermute | solution.py:388
  413.0 253.6 %reduce-scatter.3.cloned.1.call-start = ((), (), s32[]{:S(2)}) async-start(), calls=%async_computation.10 | async-start | bytes 3932160 | tf_op jit(solution)/shard_map/reduce_scatter | solution.py:380
  420.0 138.2 %collective-permute-start.56 = (bf16[768,1536]{1,0:T(8,128)(2,1)}, bf16[768,1536]{1,0:T(8,128)(2,1)}, u32[]{:S(2)}, u32[]{:S(2)}) collective-permute-start(bf16[768,1536]{1,0:T(8,128)(2,1)} %select_convert_fusion), channel_id=1, source_target_pairs={{0,8},{8,0},{1,9},{9,1},{2,10},{10,2},{3,11},{11,3},{4,12},{12,4},... | collective-permute-start | bytes 7077896 | tf_op jit(solution)/shard_map/ppermute | solution.py:388
  498.3 78.4 %collective-permute-start.47 = (bf16[128,1536]{1,0:T(8,128)(2,1)}, bf16[128,1536]{1,0:T(8,128)(2,1)S(1)}, u32[]{:S(2)}, u32[]{:S(2)}) collective-permute-start(bf16[128,1536]{1,0:T(8,128)(2,1)} %get-tuple-element.66), channel_id=1, source_target_pairs={{0,1},{1,0},{2,3},{3,2},{4,5},{5,4},{6,7},{7,6},{8,9},{9,8},{10,11... | collective-permute-start | bytes 1179656 | tf_op jit(solution)/shard_map/ppermute | solution.py:388
  500.3 45.3 %collective-permute-start.49 = (bf16[128,1536]{1,0:T(8,128)(2,1)S(1)}, bf16[128,1536]{1,0:T(8,128)(2,1)S(1)}, u32[]{:S(2)}, u32[]{:S(2)}) collective-permute-start(bf16[128,1536]{1,0:T(8,128)(2,1)S(1)} %get-tuple-element.68), channel_id=1, source_target_pairs={{0,1},{1,0},{2,3},{3,2},{4,5},{5,4},{6,7},{7,6},{8,9},{9,8},{10,11... | collective-permute-start | bytes 1179656 | tf_op jit(solution)/shard_map/ppermute | solution.py:388
  501.8 50.4 %collective-permute-start.48 = (bf16[128,1536]{1,0:T(8,128)(2,1)S(1)}, bf16[128,1536]{1,0:T(8,128)(2,1)}, u32[]{:S(2)}, u32[]{:S(2)}) collective-permute-start(bf16[128,1536]{1,0:T(8,128)(2,1)S(1)} %get-tuple-element.69), channel_id=1, source_target_pairs={{0,1},{1,0},{2,3},{3,2},{4,5},{5,4},{6,7},{7,6},{8,9},{9,8},{10,11... | collective-permute-start | bytes 1179656 | tf_op jit(solution)/shard_map/ppermute | solution.py:388
  519.7 25.9 %collective-permute-start.51 = (bf16[128,1536]{1,0:T(8,128)(2,1)}, bf16[128,1536]{1,0:T(8,128)(2,1)S(1)}, u32[]{:S(2)}, u32[]{:S(2)}) collective-permute-start(bf16[128,1536]{1,0:T(8,128)(2,1)} %fusion.31), channel_id=1, source_target_pairs={{0,2},{2,4},{4,6},{6,0},{1,3},{3,5},{5,7},{7,1},{8,10},{10,12},{12... | collective-permute-start | bytes 1179656 | tf_op jit(solution)/shard_map/ppermute | solution.py:393
  552.2 26.2 %collective-permute-start.54 = (bf16[2,384,1152]{2,1,0:T(8,128)(2,1)}, bf16[2,384,1152]{2,1,0:T(8,128)(2,1)S(1)}, u32[]{:S(2)}, u32[]{:S(2)}) collective-permute-start(bf16[2,384,1152]{2,1,0:T(8,128)(2,1)} %fusion.1), channel_id=1, source_target_pairs={{0,8},{8,0},{1,9},{9,1},{2,10},{10,2},{3,11},{11,3},{4,12},{12,4},... | collective-permute-start | bytes 5308424 | tf_op jit(solution)/shard_map/ppermute | solution.py:388
  565.3 30.2 %collective-permute-start.57 = (bf16[384,1536]{1,0:T(8,128)(2,1)}, bf16[384,1536]{1,0:T(8,128)(2,1)}, u32[]{:S(2)}, u32[]{:S(2)}) collective-permute-start(bf16[384,1536]{1,0:T(8,128)(2,1)} %select_convert_fusion.2), channel_id=1, source_target_pairs={{0,16},{16,0},{1,17},{17,1},{2,18},{18,2},{3,19},{19,3},{4,20},{20... | collective-permute-start | bytes 3538952 | tf_op jit(solution)/shard_map/ppermute | solution.py:388
  599.4 21.0 %collective-permute-start.55 = (bf16[384,1152]{1,0:T(8,128)(2,1)S(1)}, bf16[384,1152]{1,0:T(8,128)(2,1)S(1)}, u32[]{:S(2)}, u32[]{:S(2)}) collective-permute-start(bf16[384,1152]{1,0:T(8,128)(2,1)S(1)} %fusion.3), channel_id=1, source_target_pairs={{0,16},{16,0},{1,17},{17,1},{2,18},{18,2},{3,19},{19,3},{4,20},{20... | collective-permute-start | bytes 2654216 | tf_op jit(solution)/shard_map/ppermute | solution.py:388
  621.5 45.0 %all-to-all-start.4 = ((bf16[8,48,1152]{2,1,0:T(8,128)(2,1)}), bf16[8,48,1152]{2,1,0:T(8,128)(2,1)}, u32[]{:S(2)}, u32[]{:S(2)}) async-start(bf16[8,48,1152]{2,1,0:T(8,128)(2,1)} %bitcast.102), calls=%async_computation.4 | async-start | bytes 1769472 | tf_op jit(solution)/shard_map/all_to_all | solution.py:384
  625.8 32.7 %collective-permute-start.60 = (bf16[48,1536]{1,0:T(8,128)(2,1)S(1)}, bf16[48,1536]{1,0:T(8,128)(2,1)S(1)}, u32[]{:S(2)}, u32[]{:S(2)}) collective-permute-start(bf16[48,1536]{1,0:T(8,128)(2,1)S(1)} %fusion.47), channel_id=1, source_target_pairs={{0,2},{2,4},{4,6},{6,0},{1,3},{3,5},{5,7},{7,1},{8,10},{10,12},{12... | collective-permute-start | bytes 442376 | tf_op jit(solution)/shard_map/ppermute | solution.py:393
  (88 other events, 1057.2 us)
Sparse Core Ops, SparseCore 0:
  27.4 101.4 all-gather.2
  130.4 35.0 all-gather.4
  355.1 34.1 reduce-scatter.4
  574.8 74.7 reduce-scatter.2
